TPU v7x, 128 devices: a whole 4x4x4 slice. The times are simulated.
128 devices in a mesh: grp: 16 (over z, y_hi, core), brk: 8 (over y_lo, x).
Axes of the slice: x: 4, y: 4 (y_hi: 2, y_lo: 2; y = y_hi * 2 + y_lo), z: 4, core: 2. Of those that a mesh axis runs over, the one named last changes fastest.
Arguments:
- state: float32 [16, 5, 384, 64, 128], P('grp', None, 'brk'), may hold values from -6 to 6
- adjoint: float32 [16, 5, 384, 64, 128], P('grp', None, 'brk'), may hold values from -6 to 6
- source: float32 [16, 5, 384, 64, 128], P('grp', None, 'brk'), may hold values from -6 to 6
- kappa: float32 [16, 384, 64, 128], P('grp', 'brk'), may hold values from 0.2 to 3
- cut_flags: int32 [16, 384, 64, 128], P('grp', 'brk'), may hold values 0 or 1
- coupling: float32 [5, 5], replicated, may hold values from -2.5 to 2.5
- target: int32 [128, 128], replicated, may hold values from 0 to 16383, as said below
Outputs:
- estimate: float32 [16384, 5, 384], P(('grp', 'brk'))
Inputs may be any that keep to these rules, and one draw needn't show every extreme that they name: `target`: each value owner * 128 + slot appears exactly once; the owner is never in the sender's own level group; a brick sends at most 2 tiles to one owner, and exactly 2 to some owners.
All inputs are finite; a program needn't handle non-finite values. No bound on the sum of `cut_flags` on one device may be relied on, other than what follows from the above.
Results may differ from a plain program's by a relative error of at most 0.00007.
Values sent between devices are 32-bit elements; how exact they have to be, the bound alone decides.
No kernel may reach another device: no remote copies, remote signals or barrier semaphores. Data moves between devices by JAX's collectives and lax.ppermute only.
A program may use at most 512 MiB of HBM per device.

v0:
```python
import jax
import jax.numpy as jnp
from jax import lax
from jax.sharding import PartitionSpec as P


def with_halo(x, sides, width):
    for axis, dim in sides:
        size, length = (lax.axis_size(axis), x.shape[dim])
        up = [(i, (i + 1) % size) for i in range(size - 1)]
        down = [(j, i) for i, j in up]
        last = lax.slice_in_dim(x, length - width, length, axis=dim)
        initial = lax.slice_in_dim(x, 0, width, axis=dim)
        before = lax.ppermute(last, axis, up)
        after = lax.ppermute(initial, axis, down)
        x = jnp.concatenate([before, x, after], axis=dim)
    return x


def cut_along(x, dim, length):
    before, after = (x.shape[:dim], x.shape[dim + 1 :])
    return jnp.moveaxis(x.reshape(*before, length, -1, *after), dim, 0)


def in_order(parts, dim):
    parts = jnp.moveaxis(parts, 0, dim)
    shape = parts.shape
    return parts.reshape(*shape[:dim], shape[dim] * shape[dim + 1], *shape[dim + 2 :])


def joined_exchange(x, axis, axes, splits, concats):
    sizes = [lax.axis_size(a) for a in axes]
    parts = cut_along(x, splits[0], sizes[0])
    parts = jnp.moveaxis(cut_along(parts, splits[1] + 1, sizes[1]), 0, 1)
    inside = parts.shape[2:]
    parts = parts.reshape(-1, *inside)
    parts = lax.all_to_all(parts, axis, split_axis=0, concat_axis=0, tiled=True)
    parts = in_order(parts.reshape(*sizes, *inside), concats[0] + 1)
    return in_order(parts, concats[1])


def local(state, adjoint, source, kappa, cut_flags, coupling, target):
    values = state[0]
    fields, cells_x, cells_y, cells_z = values.shape
    framed = with_halo(values, (("brk", 1),), 1)
    framed = jnp.pad(framed, ((0, 0), (0, 0), (1, 1), (1, 1)))
    neighbours = framed[:, 2:, 1:-1, 1:-1] + framed[:, :-2, 1:-1, 1:-1]
    neighbours = neighbours + framed[:, 1:-1, 2:, 1:-1] + framed[:, 1:-1, :-2, 1:-1]
    neighbours = neighbours + framed[:, 1:-1, 1:-1, 2:] + framed[:, 1:-1, 1:-1, :-2]
    coupled = jnp.einsum("fg,gxyz->fxyz", coupling, values, precision=lax.Precision.HIGHEST)
    residual = source[0] - ((6.0 + kappa[0][None]) * values - neighbours + coupled)
    weighted = (1.0 - 0.5 * cut_flags[0].astype(jnp.float32))[None] * adjoint[0] * residual
    groups = lax.axis_size("grp")
    bricks = lax.axis_size("brk")
    owners = groups * bricks
    per_dev = target.shape[1]
    capacity = per_dev // ((groups - 1) * bricks) + 1
    tile_len = cells_x * cells_y * cells_z // 8 // per_dev
    slots_all = owners * capacity
    blocks = weighted.reshape(fields, cells_x // 2, 2, cells_y // 2, 2, cells_z // 2, 2).sum(
        axis=(2, 4, 6)
    )
    pieces = blocks.reshape(fields, per_dev, tile_len)
    myself = lax.axis_index(("grp", "brk"))
    owner_all = target // per_dev
    slot_all = target % per_dev
    tile_rows = lax.broadcasted_iota(jnp.int32, (per_dev, per_dev), 0)
    tile_cols = lax.broadcasted_iota(jnp.int32, (per_dev, per_dev), 1)
    earlier = tile_cols < tile_rows
    same_owner = owner_all[:, :, None] == owner_all[:, None, :]
    rank_all = jnp.sum(jnp.logical_and(same_owner, earlier[None]), axis=2)
    my_owner = lax.dynamic_index_in_dim(owner_all, myself, 0, keepdims=False)
    my_rank = lax.dynamic_index_in_dim(rank_all, myself, 0, keepdims=False)
    send_slot = my_owner * capacity + my_rank
    slot_line = jnp.arange(slots_all, dtype=jnp.int32)
    send_mat = (slot_line[:, None] == send_slot[None, :]).astype(jnp.float32)
    outgoing = jnp.einsum("ot,ftc->foc", send_mat, pieces, precision=lax.Precision.HIGHEST)
    sectioned = outgoing.reshape(fields, groups, bricks, capacity, tile_len)
    incoming = joined_exchange(sectioned, ("grp", "brk"), ("grp", "brk"), (1, 2), (1, 2))
    incoming = incoming.reshape(fields, slots_all, tile_len)
    sources = jnp.arange(owners, dtype=jnp.int32)[:, None]
    position = (sources * capacity + rank_all).reshape(-1)
    landing = jnp.where(owner_all == myself, slot_all, per_dev).reshape(-1)
    slot_ids = jnp.arange(per_dev, dtype=jnp.int32)
    matches = landing[None, :] == slot_ids[:, None]
    lookup = jnp.sum(jnp.where(matches, position[None, :], 0), axis=1)
    recv_mat = (lookup[:, None] == slot_line[None, :]).astype(jnp.float32)
    return jnp.einsum("tp,fpc->tfc", recv_mat, incoming, precision=lax.Precision.HIGHEST)


def solution(mesh):
    placed = (
        P("grp", None, "brk", None, None),
        P("grp", None, "brk", None, None),
        P("grp", None, "brk", None, None),
        P("grp", "brk", None, None),
        P("grp", "brk", None, None),
        P(),
        P(),
    )
    return jax.shard_map(
        local, mesh=mesh, in_specs=placed, out_specs=P(("grp", "brk"), None, None), check_vma=False
    )
```

profile of v0, /device:TPU:1, one launch (start us, length us, event | category | flops | bytes accessed | tf_op | source)
XLA Modules:
  0.0 409.4 jit_solution(7288584206324675873)
XLA Ops:
  0.0 10.7 %copy.34 = f32[1,5,48,64,128]{4,1,3,2,0:T(8,128)S(1)} copy(f32[1,5,48,64,128]{4,3,2,1,0:T(8,128)} %param.7) | data formatting | bytes 15728640 | tf_op args[0]
  10.7 4.5 %copy-done.2 = f32[1,5,48,64,128]{4,1,3,2,0:T(8,128)} copy-done((f32[1,5,48,64,128]{4,1,3,2,0:T(8,128)}, f32[1,5,48,64,128]{4,1,3,2,0:T(8,128)S(1)}, u32[]{:S(2)}) %copy-start.2) | copy-done | bytes 7864344
  15.2 0.8 fusion.20
  16.0 1.3 collective-permute-start
  17.3 5.3 %collective-permute-start.1 = (f32[5,1,64,128]{3,0,2,1:T(8,128)}, f32[5,1,64,128]{3,0,2,1:T(8,128)}, u32[]{:S(2)}, u32[]{:S(2)}) collective-permute-start(f32[5,1,64,128]{3,0,2,1:T(8,128)} %get-tuple-element.5), channel_id=1, source_target_pairs={{0,1},{1,2},{2,3},{3,4},{4,5},{5,6},{6,7},{8,9},{9,10},{10,11},{11... | collective-permute-start | bytes 491528 | tf_op jit(solution)/shard_map/ppermute | solution.py:14
  22.7 2.0 add_bitcast_fusion
  24.7 0.7 fusion.14
  25.4 5.1 %convert_reduce_fusion = s32[128,128]{1,0:T(8,128)S(1)} fusion(s32[128,128]{1,0:T(8,128)S(1)} %get-tuple-element.8, pred[128,128]{1,0:T(8,128)(4,1)S(1)} %iota_compare_fusion.7), kind=kLoop, calls=%fused_computation.23 | loop fusion | flops 8372224 | bytes 147456 | tf_op jit(solution)/shard_map/reduce_sum | solution.py:71
  30.5 0.6 copy-done.7
  31.1 0.5 add_bitcast_fusion.2
  31.7 19.5 %select_maximum_fusion = f32[5,50,66,130]{3,0,2,1:T(8,128)} fusion(f32[5,1,64,128]{3,0,2,1:T(8,128)S(1)} %collective-permute-done, f32[5,48,64,128]{3,0,2,1:T(8,128)} %bitcast.55, f32[5,1,64,128]{3,0,2,1:T(8,128)} %collective-permute-done.1), kind=kLoop, calls=%fused_computation.4 | loop fusion | flops 32175000 | bytes 16772000 | tf_op jit(solution)/shard_map/concatenate | solution.py:16
  51.2 64.2 %fusion.6 = f32[5,48,64,128]{3,0,2,1:T(8,128)} fusion(f32[5,50,66,130]{3,0,2,1:T(8,128)} %select_maximum_fusion, f32[5,48,64,128]{3,0,2,1:T(8,128)} %bitcast.56, f32[5,1,64,128]{3,0,2,1:T(8,128)} %collective-permute-done.1, f32[5,1,64,128]{3,0,2,1:T(8,128)S(1)} %collective-permute-done, f32[1,5,48,64,128]{4,3,2,1,0:T(8,128)} %param.9, ...), kind=kOutput, calls=%fused_computation.13 | convolution fusion | flops 143523840 | bytes 102662240 | tf_op jit(solution)/shard_map/fg,gxyz->fxyz/dot_general | solution.py:50
  115.4 87.6 %copy.25 = f32[5,48,64,128]{0,3,2,1:T(8,128)} copy(f32[5,48,64,128]{3,0,2,1:T(8,128)} %fusion.6) | data formatting | bytes 15728640 | tf_op jit(solution)/shard_map/mul | solution.py:52
  203.0 136.1 %reduce_sum.29 = f32[5,24,32,64]{0,3,2,1:T(8,128)} reduce(f32[5,24,2,32,2,64,2]{0,6,5,4,3,2,1:T(2,128)} %bitcast.10, f32[]{:T(128)} %constant.57.clone.1), dimensions={2,4,6}, to_apply=%region_2.3 | reduce | flops 1720320 | bytes 8847364 | tf_op jit(solution)/shard_map/reduce_sum | solution.py:60
  339.1 15.1 %copy.26 = f32[5,128,384]{2,1,0:T(8,128)S(1)} copy(f32[5,128,384]{0,2,1:T(8,128)} %bitcast.53) | data formatting | bytes 1966080 | tf_op jit(solution)/shard_map/reshape | solution.py:63
  354.2 0.9 convolution_bitcast_fusion
  355.2 2.4 reshape_reshape.6
  357.6 3.5 copy.27
  361.1 12.8 %all-to-all-start = ((f32[128,5,1,1,2,384]{5,4,1,3,2,0:T(2,128)}), f32[128,5,1,1,2,384]{5,4,1,3,2,0:T(2,128)S(1)}, u32[]{:S(2)}, u32[]{:S(2)}) async-start(f32[128,5,1,1,2,384]{5,4,1,3,2,0:T(2,128)} %bitcast.58), calls=%async_computation | async-start | bytes 3932160 | tf_op jit(solution)/shard_map/all_to_all | solution.py:37
  374.1 0.9 select_reduce_fusion
  375.0 28.0 %all-to-all-done = f32[128,5,1,1,2,384]{5,4,1,3,2,0:T(2,128)S(1)} async-done(((f32[128,5,1,1,2,384]{5,4,1,3,2,0:T(2,128)}), f32[128,5,1,1,2,384]{5,4,1,3,2,0:T(2,128)S(1)}, u32[]{:S(2)}, u32[]{:S(2)}) %all-to-all-start) | async-done | bytes 1966112 | tf_op jit(solution)/shard_map/all_to_all | solution.py:37
  402.9 2.0 copy.35
  405.0 2.6 reshape_reshape.7
  407.6 1.8 fusion.9
  (27 shorter events, 0.1 us)
Async XLA Ops:
  0.0 51.2 %copy-start = (f32[5,5]{1,0:T(8,128)S(1)}, f32[5,5]{1,0:T(8,128)}, u32[]{:S(2)}) copy-start(f32[5,5]{1,0:T(8,128)} %param.12) | copy-start | bytes 304
  0.0 22.6 %copy-start.3 = (f32[1,48,64,128]{3,2,1,0:T(8,128)S(1)}, f32[1,48,64,128]{3,2,1,0:T(8,128)}, u32[]{:S(2)}) copy-start(f32[1,48,64,128]{3,2,1,0:T(8,128)} %param.10) | copy-start | bytes 4718596
  0.0 22.7 %copy-start.4 = (s32[1,48,64,128]{3,2,1,0:T(8,128)S(1)}, s32[1,48,64,128]{3,2,1,0:T(8,128)}, u32[]{:S(2)}) copy-start(s32[1,48,64,128]{3,2,1,0:T(8,128)} %param.11) | copy-start | bytes 4718596
  0.0 24.7 %copy-start.10 = (s32[128,128]{1,0:T(8,128)S(1)}, s32[128,128]{1,0:T(8,128)}, u32[]{:S(2)}) copy-start(s32[128,128]{1,0:T(8,128)} %param.13) | copy-start | bytes 196612
  10.7 4.5 %copy-start.2 = (f32[1,5,48,64,128]{4,1,3,2,0:T(8,128)}, f32[1,5,48,64,128]{4,1,3,2,0:T(8,128)S(1)}, u32[]{:S(2)}) copy-start(f32[1,5,48,64,128]{4,1,3,2,0:T(8,128)S(1)} %copy.34) | copy-start | bytes 23592964
  16.0 15.6 %collective-permute-start = (f32[5,1,64,128]{3,0,2,1:T(8,128)}, f32[5,1,64,128]{3,0,2,1:T(8,128)S(1)}, u32[]{:S(2)}, u32[]{:S(2)}) collective-permute-start(f32[5,1,64,128]{3,0,2,1:T(8,128)} %get-tuple-element.6), channel_id=1, source_target_pairs={{1,0},{2,1},{3,2},{4,3},{5,4},{6,5},{7,6},{9,8},{10,9},{11,10},{12... | collective-permute-start | bytes 491528 | tf_op jit(solution)/shard_map/ppermute | solution.py:15
  17.3 14.3 %collective-permute-start.1 = (f32[5,1,64,128]{3,0,2,1:T(8,128)}, f32[5,1,64,128]{3,0,2,1:T(8,128)}, u32[]{:S(2)}, u32[]{:S(2)}) collective-permute-start(f32[5,1,64,128]{3,0,2,1:T(8,128)} %get-tuple-element.5), channel_id=1, source_target_pairs={{0,1},{1,2},{2,3},{3,4},{4,5},{5,6},{6,7},{8,9},{9,10},{10,11},{11... | collective-permute-start | bytes 491528 | tf_op jit(solution)/shard_map/ppermute | solution.py:14
  30.5 0.6 copy-start.7
  31.6 19.5 %copy-start.5 = (f32[48,64,128]{2,1,0:T(8,128)S(1)}, f32[48,64,128]{2,1,0:T(8,128)}, u32[]{:S(2)}) copy-start(f32[48,64,128]{2,1,0:T(8,128)} %get-tuple-element.9) | copy-start | bytes 4718596
  31.6 19.5 %copy-start.6 = (f32[48,64,128]{2,1,0:T(8,128)S(1)}, f32[48,64,128]{2,1,0:T(8,128)}, u32[]{:S(2)}) copy-start(f32[48,64,128]{2,1,0:T(8,128)} %get-tuple-element.10) | copy-start | bytes 4718596
  339.1 15.1 %copy-start.11 = (s32[128]{0:T(128)S(1)}, s32[128]{0:T(128)}, u32[]{:S(2)}) copy-start(s32[128]{0:T(128)} %add_bitcast_fusion.2) | copy-start | bytes 1540
  339.1 70.3 %copy-start.1 = (f32[5,5]{1,0:T(8,128)S(1)}, f32[5,5]{1,0:T(8,128)}, u32[]{:S(2)}) copy-start(f32[5,5]{1,0:T(8,128)} %param.12) | copy-start | bytes 304
  354.2 19.7 %copy-start.8 = (s32[128,128]{1,0:T(8,128)S(1)}, s32[128,128]{1,0:T(8,128)}, u32[]{:S(2)}) copy-start(s32[128,128]{1,0:T(8,128)} %copy-done.7) | copy-start | bytes 196612
  354.2 19.8 %copy-start.9 = (s32[16384]{0:T(1024)S(1)}, s32[16384]{0:T(1024)}, u32[]{:S(2)}) copy-start(s32[16384]{0:T(1024)} %get-tuple-element.7) | copy-start | bytes 196612
  361.1 41.8 %all-to-all-start = ((f32[128,5,1,1,2,384]{5,4,1,3,2,0:T(2,128)}), f32[128,5,1,1,2,384]{5,4,1,3,2,0:T(2,128)S(1)}, u32[]{:S(2)}, u32[]{:S(2)}) async-start(f32[128,5,1,1,2,384]{5,4,1,3,2,0:T(2,128)} %bitcast.58), calls=%async_computation | async-start | bytes 3932160 | tf_op jit(solution)/shard_map/all_to_all | solution.py:37
where the time goes:
time: 411 us; the launch traced here: 409 us
  other arithmetic  165 us (40%)
  local copies, waits for them, and re-layouts  130 us (32%)
  matrix products  67 us (16%)
  waiting for transfers between devices  28 us (7%)
  starting transfers between devices  19.4 us (5%)
    reduce_sum x1, other arithmetic, local(): weighted.reshape(fields, cells_x // 2, 2, cells_y // 2, 2, cells_z // 2, 2)  136 us
    mul x1, local copies, waits for them, and re-layouts, local(): (1.0 - 0.5 * cut_flags[0].astype(jnp.float32))[None] * adjoint[0] * residual  87.6 us
    dot_general x1, matrix products, local(): jnp.einsum('fg,gxyz->fxyz', coupling, values, precision=lax.Precision.HIG...  64.2 us
    all_to_all x1, waiting for transfers between devices, joined_exchange(): parts = lax.all_to_all(parts, axis, split_axis=0, concat_axis=0, tiled=True)  28 us
    concatenate x1, other arithmetic, with_halo(): x = jnp.concatenate([before, x, after], axis=dim)  19.5 us
    unnamed x25, local copies, waits for them, and re-layouts  15.8 us
    reshape x1, local copies, waits for them, and re-layouts, local(): pieces = blocks.reshape(fields, per_dev, tile_len)  15.1 us
    all_to_all x1, starting transfers between devices, joined_exchange(): parts = lax.all_to_all(parts, axis, split_axis=0, concat_axis=0, tiled=True)  12.8 us
  transfers between devices with their start and end apart: 3, of which 1 were waited for; matrix products, arithmetic and copies ran while one was open for 2% of the time, Pallas kernels for 0%

commit v1 on v0

v1 whole, which is shorter than its diff:
```python
import functools
import jax
import jax.numpy as jnp
from jax import lax
from jax.experimental import pallas as pl
from jax.experimental.pallas import tpu as pltpu
from jax.sharding import PartitionSpec as P

VMEM_LIMIT = 56 * 1024 * 1024
AHEAD = 5


def weight_of(flags):
    return 1.0 - 0.5 * flags.astype(jnp.float32)


def pool_matrix(lanes):
    row = lax.broadcasted_iota(jnp.int32, (2 * lanes, lanes), 0)
    col = lax.broadcasted_iota(jnp.int32, (2 * lanes, lanes), 1)
    return jnp.where(row // 2 == col, 1.0, 0.0).astype(jnp.bfloat16)


def pooled_rows(fine_ref, fields, cells_y, matrix):
    rows = cells_y // 4
    parts = [[fine_ref[f, pl.ds(k, rows, stride=4), :] for k in range(4)] for f in range(fields)]
    low = jnp.concatenate([p[0] + p[1] for p in parts], axis=0)
    high = jnp.concatenate([p[2] + p[3] for p in parts], axis=0)
    both = jnp.concatenate([low, high], axis=1)
    first = both.astype(jnp.bfloat16)
    rest = both - first.astype(jnp.float32)
    second = rest.astype(jnp.bfloat16)
    dot = functools.partial(jnp.dot, preferred_element_type=jnp.float32)
    return dot(first, matrix) + dot(second, matrix)


def main_kernel(state, adjoint, source, kappa, flags, coupling, out, sv, av, bv, kv, fv, wv, pv, sems):
    fields, cells_x, cells_y, lanes = adjoint.shape
    steps = cells_x // 2
    rows = cells_y // 4

    def copy(step, i):
        at = pl.ds(2 * step, 2)
        if i == 0:
            landing = sv.at[:, pl.ds(2 * step + 1, 2), pl.ds(8, cells_y)]
            return pltpu.make_async_copy(state.at[:, at], landing, sems.at[step, 0])
        if i < 3:
            src, dst = ((adjoint, av), (source, bv))[i - 1]
            return pltpu.make_async_copy(src.at[:, at], dst.at[:, at], sems.at[step, i])
        src, dst = ((kappa, kv), (flags, fv))[i - 3]
        return pltpu.make_async_copy(src.at[at], dst.at[at], sems.at[step, i])

    def start(step):
        for i in range(5):
            copy(step, i).start()

    for step in range(AHEAD):
        start(step)
    zero = jnp.zeros((8, lanes), jnp.float32)
    pv[...] = pool_matrix(lanes)

    def clear(x, carry):
        for f in range(fields):
            sv[f, x, pl.ds(0, 8), :] = zero
            sv[f, x, pl.ds(cells_y + 8, 8), :] = zero
        return carry

    lax.fori_loop(0, cells_x + 2, clear, 0)
    for f in range(fields):
        for y in range(0, cells_y, 8):
            sv[f, 0, pl.ds(y + 8, 8), :] = zero
            sv[f, cells_x + 1, pl.ds(y + 8, 8), :] = zero

    coef = [[coupling[f, h] for h in range(fields)] for f in range(fields)]
    lane = lax.broadcasted_iota(jnp.int32, (8, lanes), 1)
    inner_lo = lane != 0
    inner_hi = lane != lanes - 1
    copy(0, 0).wait()

    def step_body(step, carry):
        @pl.when(step + AHEAD < steps)
        def _():
            start(step + AHEAD)

        @pl.when(step + 1 < steps)
        def _():
            copy(step + 1, 0).wait()

        for i in range(1, 5):
            copy(step, i).wait()

        for y in range(0, cells_y, 8):
            total = [None] * fields
            for p in range(2):
                x = 2 * step + p
                kap = kv[x, pl.ds(y, 8), :]
                wgt = weight_of(fv[x, pl.ds(y, 8), :])
                mid = [sv[f, x + 1, pl.ds(y + 8, 8), :] for f in range(fields)]
                for f in range(fields):
                    near = sv[f, x, pl.ds(y + 8, 8), :] + sv[f, x + 2, pl.ds(y + 8, 8), :]
                    near = near + sv[f, x + 1, pl.ds(y + 7, 8), :] + sv[f, x + 1, pl.ds(y + 9, 8), :]
                    near = near + jnp.where(inner_lo, pltpu.roll(mid[f], 1, 1), 0.0)
                    near = near + jnp.where(inner_hi, pltpu.roll(mid[f], lanes - 1, 1), 0.0)
                    applied = (kap + (coef[f][f] + 6.0)) * mid[f]
                    for h in range(fields):
                        if h != f:
                            applied = applied + coef[f][h] * mid[h]
                    residual = bv[f, x, pl.ds(y, 8), :] - applied + near
                    term = wgt * av[f, x, pl.ds(y, 8), :] * residual
                    total[f] = term if p == 0 else total[f] + term
            for f in range(fields):
                wv[f, pl.ds(y, 8), :] = total[f]
        pooled = pooled_rows(wv, fields, cells_y, pv[...])
        for f in range(fields):
            out[f, pl.ds(pl.multiple_of(step * rows, rows), rows), :] = pooled[f * rows : (f + 1) * rows]
        return carry

    lax.fori_loop(0, steps, step_body, 0)


def main_part(state, adjoint, source, kappa, flags, coupling):
    fields, cells_x, cells_y, lanes = state.shape
    f32 = jnp.float32
    anyspace = pl.BlockSpec(memory_space=pl.ANY)
    return pl.pallas_call(
        main_kernel,
        out_shape=jax.ShapeDtypeStruct((fields, cells_x * cells_y // 8, lanes), f32),
        in_specs=[anyspace] * 5 + [pl.BlockSpec(memory_space=pltpu.SMEM)],
        out_specs=pl.BlockSpec(memory_space=pltpu.VMEM),
        scratch_shapes=[
            pltpu.VMEM((fields, cells_x + 2, cells_y + 16, lanes), f32),
            pltpu.VMEM((fields, cells_x, cells_y, lanes), f32),
            pltpu.VMEM((fields, cells_x, cells_y, lanes), f32),
            pltpu.VMEM((cells_x, cells_y, lanes), f32),
            pltpu.VMEM((cells_x, cells_y, lanes), jnp.int32),
            pltpu.VMEM((fields, cells_y, lanes), f32),
            pltpu.VMEM((2 * lanes, lanes), jnp.bfloat16),
            pltpu.SemaphoreType.DMA((cells_x // 2, 5)),
        ],
        compiler_params=pltpu.CompilerParams(vmem_limit_bytes=VMEM_LIMIT),
        cost_estimate=pl.CostEstimate(flops=100_000_000, bytes_accessed=27_700_000, transcendentals=0),
        name="residual_pool",
    )(state, adjoint, source, kappa, flags, coupling)


def pack_kernel(capacity, tiles, part, before, after, adj_lo, adj_hi, flag_lo, flag_hi, out, wv, pv, slots, seen):
    fields, cells_y, lanes = before.shape
    rows = cells_y // 4
    per_dev = tiles.shape[1]
    cells = part.shape[1]
    span = cells // per_dev

    def clear(i, carry):
        seen[i] = 0
        return carry

    lax.fori_loop(0, per_dev, clear, 0)

    def rank(t, carry):
        owner = lax.shift_right_logical(tiles[0, t], per_dev.bit_length() - 1)
        count = seen[owner]
        slots[t] = (owner * capacity + count) * (span * fields)
        seen[owner] = count + 1
        return carry

    lax.fori_loop(0, per_dev, rank, 0)
    pv[...] = pool_matrix(lanes)
    for face, dual, flag, at in ((before, adj_lo, flag_lo, 0), (after, adj_hi, flag_hi, cells - rows)):
        for y in range(0, cells_y, 8):
            wgt = weight_of(flag[0, pl.ds(y, 8), :])
            for f in range(fields):
                wv[f, pl.ds(y, 8), :] = wgt * dual[f, 0, pl.ds(y, 8), :] * face[f, pl.ds(y, 8), :]
        pooled = pooled_rows(wv, fields, cells_y, pv[...])
        for f in range(fields):
            part[f, pl.ds(at, rows), :] = part[f, pl.ds(at, rows), :] + pooled[f * rows : (f + 1) * rows]

    def place(t, carry):
        base = slots[t]
        for f in range(fields):
            for j in range(span):
                out[pl.ds(base + f * span + j, 1), :] = part[f, pl.ds(t * span + j, 1), :]
        return carry

    lax.fori_loop(0, per_dev, place, 0)


def pack_part(part, before, after, adjoint, flags, tiles, capacity, owners):
    fields, cells_x, cells_y, lanes = adjoint.shape
    per_dev = tiles.shape[1]
    span = part.shape[1] // per_dev
    f32 = jnp.float32

    def plane(x):
        return pl.BlockSpec((fields, 1, cells_y, lanes), lambda i: (0, x, 0, 0))

    def flag_plane(x):
        return pl.BlockSpec((1, cells_y, lanes), lambda i: (x, 0, 0))

    def whole(a):
        return pl.BlockSpec(a.shape, lambda i: (0,) * a.ndim)

    def body(tiles, part_in, *refs):
        part_ref = refs[-1]
        part_ref[...] = part_in[...]
        pack_kernel(capacity, tiles, part_ref, *refs[:-1])

    n_rows = owners * capacity * span * fields
    return pl.pallas_call(
        body,
        grid=(1,),
        out_shape=jax.ShapeDtypeStruct((n_rows, lanes), f32),
        in_specs=[
            pl.BlockSpec(memory_space=pltpu.SMEM),
            whole(part),
            whole(before),
            whole(after),
            plane(0),
            plane(cells_x - 1),
            flag_plane(0),
            flag_plane(cells_x - 1),
        ],
        out_specs=pl.BlockSpec((n_rows, lanes), lambda i: (0, 0)),
        scratch_shapes=[
            pltpu.VMEM((fields, cells_y, lanes), f32),
            pltpu.VMEM((2 * lanes, lanes), jnp.bfloat16),
            pltpu.SMEM((per_dev,), jnp.int32),
            pltpu.SMEM((owners,), jnp.int32),
            pltpu.VMEM(part.shape, f32),
        ],
        compiler_params=pltpu.CompilerParams(vmem_limit_bytes=VMEM_LIMIT),
        cost_estimate=pl.CostEstimate(flops=1_000_000, bytes_accessed=3_500_000, transcendentals=0),
        name="edges_pack",
    )(tiles, part, before, after, adjoint, adjoint, flags, flags)


def unpack_kernel(lookup, received, out):
    fields, per_dev, width = out.shape
    lanes = received.shape[1]
    span = width // lanes

    sub = lax.broadcasted_iota(jnp.int32, (8, lanes), 0)

    def place(g, carry):
        bases = [lookup[g * 8 + s] * (span * fields) for s in range(8)]
        for f in range(fields):
            for j in range(span):
                rows = [received[pl.ds(b + f * span + j, 8, stride=0), :] for b in bases]
                value = rows[0]
                for s in range(1, 8):
                    value = jnp.where(sub == s, rows[s], value)
                out[f, pl.ds(pl.multiple_of(g * 8, 8), 8), pl.ds(j * lanes, lanes)] = value
        return carry

    lax.fori_loop(0, per_dev // 8, place, 0)


def unpack_part(lookup, received, fields, per_dev, width):
    vmem = pl.BlockSpec(memory_space=pltpu.VMEM)
    return pl.pallas_call(
        unpack_kernel,
        out_shape=jax.ShapeDtypeStruct((fields, per_dev, width), jnp.float32),
        in_specs=[pl.BlockSpec(memory_space=pltpu.SMEM), vmem],
        out_specs=vmem,
        compiler_params=pltpu.CompilerParams(vmem_limit_bytes=VMEM_LIMIT),
        cost_estimate=pl.CostEstimate(flops=0, bytes_accessed=3_000_000, transcendentals=0),
        name="unpack",
    )(lookup, received)


def local(state, adjoint, source, kappa, cut_flags, coupling, target):
    state, adjoint, source, kappa, flags = (a[0] for a in (state, adjoint, source, kappa, cut_flags))
    fields, cells_x, cells_y, lanes = state.shape
    groups, bricks = lax.axis_size("grp"), lax.axis_size("brk")
    owners = groups * bricks
    per_dev = target.shape[1]
    capacity = per_dev // ((groups - 1) * bricks) + 1
    width = cells_x * cells_y * lanes // 8 // per_dev
    myself = lax.axis_index(("grp", "brk"))

    up = [(i, i + 1) for i in range(bricks - 1)]
    down = [(j, i) for i, j in up]
    before = lax.ppermute(state[:, cells_x - 1], "brk", up)
    after = lax.ppermute(state[:, 0], "brk", down)

    part = main_part(state, adjoint, source, kappa, flags, coupling)
    mine = lax.dynamic_slice_in_dim(target, myself, 1, 0)
    outgoing = pack_part(part, before, after, adjoint, flags, mine, capacity, owners)
    incoming = lax.all_to_all(outgoing, ("grp", "brk"), 0, 0, tiled=True)

    slot_ids = myself * per_dev + jnp.arange(per_dev, dtype=jnp.int32)
    codes = jnp.arange(owners * per_dev, dtype=jnp.int32)
    hit = target.reshape(-1)[None, :] == slot_ids[:, None]
    origin = jnp.sum(jnp.where(hit, codes[None, :], 0), axis=1)
    sender = origin // per_dev
    before_it = jnp.logical_and(sender[:, None] == sender[None, :], origin[None, :] < origin[:, None])
    lookup = sender * capacity + jnp.sum(before_it.astype(jnp.int32), axis=1)
    out = unpack_part(lookup, incoming, fields, per_dev, width)
    return out.transpose(1, 0, 2)


def solution(mesh):
    placed = (
        P("grp", None, "brk", None, None),
        P("grp", None, "brk", None, None),
        P("grp", None, "brk", None, None),
        P("grp", "brk", None, None),
        P("grp", "brk", None, None),
        P(),
        P(),
    )
    return jax.shard_map(
        local, mesh=mesh, in_specs=placed, out_specs=P(("grp", "brk"), None, None), check_vma=False
    )
```

time: 411 us -> 83.3 us (0.20)
  other arithmetic: 165 us -> 2.02 us
  local copies, waits for them, and re-layouts: 130 us -> 10 us
  matrix products: 67 us -> 0 us
  Pallas kernels: 0 us -> 23.2 us
    reduce_sum x3 -> x2, other arithmetic: 142 us -> 1.5 us  [the longest x1 1.32 us: local(): origin = jnp.sum(jnp.where(hit, codes[None, :], 0), axis=1)]
    mul x1 -> x0, local copies, waits for them, and re-layouts: 87.6 us -> none  [local(): (1.0 - 0.5 * cut_flags[0].astype(jnp.float32))[None] * adjoint[0] * residual]
    dot_general x3 -> x0, matrix products: 67 us -> none  [the longest x1 64.2 us: local(): jnp.einsum('fg,gxyz->fxyz', coupling, values, precision=lax.Precision.HIG...]
    pallas_call x0 -> x3, Pallas kernels: none -> 23.2 us  [the longest x1 14.3 us: main_part(): pl.pallas_call(main_kernel, out_shape=jax.ShapeDtypeStruct((fields, cells...]
    concatenate x1 -> x0, other arithmetic: 19.5 us -> none  [with_halo(): x = jnp.concatenate([before, x, after], axis=dim)]
    reshape x2 -> x0, local copies, waits for them, and re-layouts: 17.1 us -> none  [the longest x1 15.1 us: local(): pieces = blocks.reshape(fields, per_dev, tile_len)]
    unnamed x25 -> x7, local copies, waits for them, and re-layouts: 15.8 us -> 5.34 us
    another operation x3 -> x0, local copies, waits for them, and re-layouts: 8.57 us -> none  [the longest x1 3.52 us: joined_exchange(): parts = jnp.moveaxis(cut_along(parts, splits[1] + 1, sizes[1]), 0, 1)]
  transfers between devices with their start and end apart: 3 -> 3, of which waited for: 1 -> 1; matrix products, arithmetic and copies ran while one was open for 2% -> 3% of each run, Pallas kernels for 0% -> 17%
where the time goes in v1:
time: 83.3 us; the launch traced here: 82.9 us
  waiting for transfers between devices  28.4 us (34%)
  Pallas kernels  23.2 us (28%)
  starting transfers between devices  19.2 us (23%)
  local copies, waits for them, and re-layouts  10 us (12%)
  other arithmetic  2.02 us (2%)
    all_to_all x1, waiting for transfers between devices, local(): incoming = lax.all_to_all(outgoing, ('grp', 'brk'), 0, 0, tiled=True)  28.4 us
    pallas_call x1, Pallas kernels, main_part(): pl.pallas_call(main_kernel, out_shape=jax.ShapeDtypeStruct((fields, cells...  14.3 us
    all_to_all x1, starting transfers between devices, local(): incoming = lax.all_to_all(outgoing, ('grp', 'brk'), 0, 0, tiled=True)  13.3 us
    pallas_call x1, Pallas kernels, pack_part(): pl.pallas_call(body, grid=(1,), out_shape=jax.ShapeDtypeStruct((n_rows, l...  5.91 us
    unnamed x7, local copies, waits for them, and re-layouts  5.34 us
    ppermute x1, starting transfers between devices, local(): before = lax.ppermute(state[:, cells_x - 1], 'brk', up)  4.58 us
    all_to_all x2, local copies, waits for them, and re-layouts, local(): incoming = lax.all_to_all(outgoing, ('grp', 'brk'), 0, 0, tiled=True)  4.09 us
    pallas_call x1, Pallas kernels, unpack_part(): pl.pallas_call(unpack_kernel, out_shape=jax.ShapeDtypeStruct((fields, per...  3.03 us
  transfers between devices with their start and end apart: 3, of which 1 were waited for; matrix products, arithmetic and copies ran while one was open for 3% of the time, Pallas kernels for 17%

profile of v1, /device:TPU:1, one launch (start us, length us, event | category | flops | bytes accessed | tf_op | source)
XLA Modules:
  0.0 82.9 jit_solution(1648042971413445519)
XLA Ops:
  0.0 4.0 %copy.16 = f32[1,5,48,64,128]{4,3,1,2,0:T(8,128)S(1)} copy(f32[1,5,48,64,128]{4,3,2,1,0:T(8,128)} %param.7) | data formatting | bytes 15728640 | tf_op args[0]
  4.0 1.3 %collective-permute-start.1 = (f32[5,64,128]{2,1,0:T(8,128)S(1)}, f32[5,64,128]{2,1,0:T(8,128)S(1)}, u32[]{:S(2)}, u32[]{:S(2)}) collective-permute-start(f32[5,64,128]{2,1,0:T(8,128)S(1)} %get-tuple-element.5), channel_id=1, source_target_pairs={{1,0},{2,1},{3,2},{4,3},{5,4},{6,5},{7,6},{9,8},{10,9},{11,10},{12... | collective-permute-start | bytes 491528 | tf_op jit(solution)/shard_map/ppermute | solution.py:282
  5.3 4.6 %collective-permute-start = (f32[5,64,128]{2,1,0:T(8,128)S(1)}, f32[5,64,128]{2,1,0:T(8,128)S(1)}, u32[]{:S(2)}, u32[]{:S(2)}) collective-permute-start(f32[5,64,128]{2,1,0:T(8,128)S(1)} %get-tuple-element.6), channel_id=1, source_target_pairs={{0,1},{1,2},{2,3},{3,4},{4,5},{5,6},{6,7},{8,9},{9,10},{10,11},{11... | collective-permute-start | bytes 491528 | tf_op jit(solution)/shard_map/ppermute | solution.py:281
  9.9 0.0 copy-start.2
  10.0 14.3 %residual_pool.1.part_in = f32[5,384,128]{2,1,0:T(8,128)} custom-call(f32[5,48,64,128]{3,2,1,0:T(8,128)} %bitcast.17, f32[5,48,64,128]{3,2,1,0:T(8,128)} %bitcast.14, f32[5,48,64,128]{3,2,1,0:T(8,128)} %bitcast.22, f32[48,64,128]{2,1,0:T(8,128)} %bitcast.23, s32[48,64,128]{2,1,0:T(8,128)} %bitcast.18, f32[5,5]{1,0:T(8,128)} %coupling.1), custom_call_target="tpu_custom_call" | custom-call | flops 100000000 | bytes 27700000 | tf_op jit(solution)/shard_map/residual_pool/pallas_call | solution.py:124
  24.2 0.0 copy-done.2
  24.3 0.6 constant_dynamic-slice_fusion.tiles
  24.8 0.0 collective-permute-done.1.refs_1_
  24.8 0.0 copy-start
  24.8 0.0 collective-permute-done.refs_0_
  24.8 0.7 copy-done
  25.5 0.0 copy-start.1
  25.5 0.7 copy-done.1
  26.1 5.9 %edges_pack.1 = f32[3840,128]{1,0:T(8,128)} custom-call(s32[1,128]{1,0:T(1,128)} %constant_dynamic-slice_fusion.tiles, f32[5,384,128]{2,1,0:T(8,128)} %residual_pool.1.part_in, f32[5,64,128]{2,1,0:T(8,128)} %copy-done.1, f32[5,64,128]{2,1,0:T(8,128)} %copy-done, f32[5,48,64,128]{3,2,1,0:T(8,128)} %bitcast.15, f32[5,48,64,128]{3,2,1,0:T(8,128)} %bitcast.16, ...), custom_call_target="tpu_custom_call" | custom-call | flops 1000000 | bytes 3500000 | tf_op jit(solution)/shard_map/edges_pack/pallas_call | solution.py:207
  32.1 2.6 %all_to_all.7 = f32[128,30,128]{2,1,0:T(8,128)} reshape(f32[3840,128]{1,0:T(8,128)} %edges_pack.1) | data formatting | bytes 3932160 | tf_op jit(solution)/shard_map/all_to_all | solution.py:287
  34.7 13.3 %all-to-all-start = ((f32[128,30,128]{2,1,0:T(8,128)}), f32[128,30,128]{2,1,0:T(8,128)S(1)}, u32[]{:S(2)}, u32[]{:S(2)}) async-start(f32[128,30,128]{2,1,0:T(8,128)} %all_to_all.7), calls=%async_computation | async-start | bytes 4194304 | tf_op jit(solution)/shard_map/all_to_all | solution.py:287
  48.0 1.3 %select_reduce_fusion = s32[128]{0:T(128)S(1)} fusion(s32[16384]{0:T(1024)S(1)} %bitcast.24, s32[128]{0:T(128)S(1)} %iota_add_fusion), kind=kLoop, calls=%fused_computation | loop fusion | flops 6291328 | bytes 66560 | tf_op jit(solution)/shard_map/reduce_sum | solution.py:292
  49.4 0.2 convert_reduce_fusion
  49.5 0.5 multiply_add_fusion.lookup
  50.1 28.4 %all-to-all-done = f32[128,30,128]{2,1,0:T(8,128)S(1)} async-done(((f32[128,30,128]{2,1,0:T(8,128)}), f32[128,30,128]{2,1,0:T(8,128)S(1)}, u32[]{:S(2)}, u32[]{:S(2)}) %all-to-all-start) | async-done | bytes 1966112 | tf_op jit(solution)/shard_map/all_to_all | solution.py:287
  78.4 1.4 %all_to_all.9.received = f32[3840,128]{1,0:T(8,128)} reshape(f32[128,30,128]{2,1,0:T(8,128)S(1)} %all-to-all-done) | data formatting | bytes 3932160 | tf_op jit(solution)/shard_map/all_to_all | solution.py:287
  79.9 3.0 %unpack.1 = f32[5,128,384]{2,1,0:T(8,128)} custom-call(s32[128]{0:T(128)} %multiply_add_fusion.lookup, f32[3840,128]{1,0:T(8,128)} %all_to_all.9.received), custom_call_target="tpu_custom_call" | custom-call | bytes 3000000 | tf_op jit(solution)/shard_map/unpack/pallas_call | solution.py:258
  (3 shorter events, 0.0 us)
Async XLA Ops:
  4.0 20.8 %collective-permute-start.1 = (f32[5,64,128]{2,1,0:T(8,128)S(1)}, f32[5,64,128]{2,1,0:T(8,128)S(1)}, u32[]{:S(2)}, u32[]{:S(2)}) collective-permute-start(f32[5,64,128]{2,1,0:T(8,128)S(1)} %get-tuple-element.5), channel_id=1, source_target_pairs={{1,0},{2,1},{3,2},{4,3},{5,4},{6,5},{7,6},{9,8},{10,9},{11,10},{12... | collective-permute-start | bytes 491528 | tf_op jit(solution)/shard_map/ppermute | solution.py:282
  5.3 19.5 %collective-permute-start = (f32[5,64,128]{2,1,0:T(8,128)S(1)}, f32[5,64,128]{2,1,0:T(8,128)S(1)}, u32[]{:S(2)}, u32[]{:S(2)}) collective-permute-start(f32[5,64,128]{2,1,0:T(8,128)S(1)} %get-tuple-element.6), channel_id=1, source_target_pairs={{0,1},{1,2},{2,3},{3,4},{4,5},{5,6},{6,7},{8,9},{9,10},{10,11},{11... | collective-permute-start | bytes 491528 | tf_op jit(solution)/shard_map/ppermute | solution.py:281
  9.9 14.3 %copy-start.2 = (s32[128,128]{1,0:T(8,128)S(1)}, s32[128,128]{1,0:T(8,128)}, u32[]{:S(2)}) copy-start(s32[128,128]{1,0:T(8,128)} %param.13) | copy-start | bytes 196612
  24.8 0.7 copy-start
  25.5 0.7 copy-start.1
  34.7 43.7 %all-to-all-start = ((f32[128,30,128]{2,1,0:T(8,128)}), f32[128,30,128]{2,1,0:T(8,128)S(1)}, u32[]{:S(2)}, u32[]{:S(2)}) async-start(f32[128,30,128]{2,1,0:T(8,128)} %all_to_all.7), calls=%async_computation | async-start | bytes 4194304 | tf_op jit(solution)/shard_map/all_to_all | solution.py:287

commit v2 on v1

v2 whole, which is shorter than its diff:
```python
import functools
import jax
import jax.numpy as jnp
from jax import lax
from jax.experimental import pallas as pl
from jax.experimental.pallas import tpu as pltpu
from jax.sharding import PartitionSpec as P

MIB = 1024 * 1024
PLANES = 4
AHEAD = 6
PAD = 8


def in_hbm(x):
    return pltpu.with_memory_space_constraint(x, pltpu.HBM)


def weight_of(flags):
    return 1.0 - 0.5 * flags.astype(jnp.float32)


def pool_matrix(lanes):
    row = lax.broadcasted_iota(jnp.int32, (2 * lanes, lanes), 0)
    col = lax.broadcasted_iota(jnp.int32, (2 * lanes, lanes), 1)
    return jnp.where(row // 2 == col, 1.0, 0.0).astype(jnp.bfloat16)


def pooled_rows(fine_ref, matrix):
    fields, cells_y, _ = fine_ref.shape
    rows = cells_y // 4
    parts = [[fine_ref[f, pl.ds(k, rows, stride=4), :] for k in range(4)] for f in range(fields)]
    low = jnp.concatenate([p[0] + p[1] for p in parts], axis=0)
    high = jnp.concatenate([p[2] + p[3] for p in parts], axis=0)
    both = jnp.concatenate([low, high], axis=1)
    first = both.astype(jnp.bfloat16)
    rest = both - first.astype(jnp.float32)
    second = rest.astype(jnp.bfloat16)
    dot = functools.partial(jnp.dot, preferred_element_type=jnp.float32)
    return dot(first, matrix) + dot(second, matrix)


def face_kernel(state, first, last, sems):
    cells_x = state.shape[1]
    one = pltpu.make_async_copy(state.at[:, 0], first, sems.at[0])
    two = pltpu.make_async_copy(state.at[:, cells_x - 1], last, sems.at[1])
    one.start()
    two.start()
    one.wait()
    two.wait()


def faces_of(state):
    fields, _, cells_y, lanes = state.shape
    face = jax.ShapeDtypeStruct((fields, cells_y, lanes), jnp.float32)
    vmem = pl.BlockSpec(memory_space=pltpu.VMEM)
    return pl.pallas_call(
        face_kernel,
        out_shape=(face, face),
        in_specs=[pl.BlockSpec(memory_space=pltpu.HBM)],
        out_specs=(vmem, vmem),
        scratch_shapes=[pltpu.SemaphoreType.DMA((2,))],
        compiler_params=pltpu.CompilerParams(vmem_limit_bytes=2 * MIB),
        cost_estimate=pl.CostEstimate(flops=0, bytes_accessed=650_000, transcendentals=0),
        name="faces",
    )(in_hbm(state))


def main_kernel(
    capacity, span, myself, coupling, target, state, adjoint, source, kv, fv,
    out, slots, sv, av, bv, wv, pv, tv, seen, sems, tsem,
):
    fields, cells_x, cells_y, lanes = adjoint.shape
    steps = cells_x // PLANES
    rows = cells_y // 4
    owners, per_dev = target.shape

    def copy(step, i):
        at = pl.ds(PLANES * step, PLANES)
        if i == 0:
            landing = sv.at[:, pl.ds(PLANES * step + 1, PLANES), pl.ds(8, cells_y)]
            return pltpu.make_async_copy(state.at[:, at], landing, sems.at[step, 0])
        src, dst = ((adjoint, av), (source, bv))[i - 1]
        return pltpu.make_async_copy(src.at[:, at], dst.at[:, at], sems.at[step, i])

    def start(step):
        for i in range(3):
            copy(step, i).start()

    me = myself[0]
    row8 = pl.multiple_of(lax.shift_left(lax.shift_right_logical(me, 3), 3), 8)
    table = pltpu.make_async_copy(target.at[pl.ds(row8, 8)], tv, tsem.at[0])
    table.start()
    for step in range(AHEAD):
        start(step)
    zero = jnp.zeros((8, lanes), jnp.float32)
    pv[...] = pool_matrix(lanes)

    def clear(x, carry):
        for f in range(fields):
            sv[f, x, pl.ds(0, 8), :] = zero
            sv[f, x, pl.ds(cells_y + 8, 8), :] = zero
        return carry

    lax.fori_loop(0, cells_x + 2, clear, 0)
    for f in range(fields):
        for y in range(0, cells_y, 8):
            sv[f, 0, pl.ds(y + 8, 8), :] = zero
            sv[f, cells_x + 1, pl.ds(y + 8, 8), :] = zero

    for i in range(owners):
        seen[i] = 0
    table.wait()
    mine = lax.bitwise_and(me, 7)

    def rank(t, carry):
        owner = lax.shift_right_logical(tv[mine, t], per_dev.bit_length() - 1)
        count = seen[owner]
        slots[t] = owner * capacity + count
        seen[owner] = count + 1
        return carry

    lax.fori_loop(0, per_dev, rank, 0, unroll=8)

    coef = [[coupling[f, h] for h in range(fields)] for f in range(fields)]
    lane = lax.broadcasted_iota(jnp.int32, (8, lanes), 1)
    inner_lo = lane != 0
    inner_hi = lane != lanes - 1

    def pool(half, at):
        pooled = pooled_rows(wv.at[half], pv[...])
        for f in range(fields):
            out[f, pl.ds(pl.multiple_of(at + PAD, 8), rows), :] = pooled[f * rows : (f + 1) * rows]

    copy(0, 0).wait()

    def step_body(step, carry):
        @pl.when(step + AHEAD < steps)
        def _():
            start(step + AHEAD)

        @pl.when(step + 1 < steps)
        def _():
            copy(step + 1, 0).wait()

        copy(step, 1).wait()
        copy(step, 2).wait()

        for half in range(PLANES // 2):
            coarse = step * (PLANES // 2) + half
            pool(1 - half % 2, jnp.maximum(coarse - 1, 0) * rows)
            for y in range(0, cells_y, 8):
                total = [None] * fields
                for p in range(2):
                    x = 2 * coarse + p
                    kap = kv[x, pl.ds(y, 8), :]
                    wgt = weight_of(fv[x, pl.ds(y, 8), :])
                    mid = [sv[f, x + 1, pl.ds(y + 8, 8), :] for f in range(fields)]
                    for f in range(fields):
                        near = sv[f, x, pl.ds(y + 8, 8), :] + sv[f, x + 2, pl.ds(y + 8, 8), :]
                        near = near + sv[f, x + 1, pl.ds(y + 7, 8), :] + sv[f, x + 1, pl.ds(y + 9, 8), :]
                        near = near + jnp.where(inner_lo, pltpu.roll(mid[f], 1, 1), 0.0)
                        near = near + jnp.where(inner_hi, pltpu.roll(mid[f], lanes - 1, 1), 0.0)
                        applied = (kap + (coef[f][f] + 6.0)) * mid[f]
                        for h in range(fields):
                            if h != f:
                                applied = applied + coef[f][h] * mid[h]
                        residual = bv[f, x, pl.ds(y, 8), :] - applied + near
                        term = wgt * av[f, x, pl.ds(y, 8), :] * residual
                        total[f] = term if p == 0 else total[f] + term
                for f in range(fields):
                    wv[half % 2, f, pl.ds(y, 8), :] = total[f]
        return carry

    lax.fori_loop(0, steps, step_body, 0)
    pool(1, (cells_x // 2 - 1) * rows)


def main_part(state, adjoint, source, kappa, flags, coupling, target, myself, capacity, span):
    fields, cells_x, cells_y, lanes = state.shape
    owners, per_dev = target.shape
    f32 = jnp.float32
    hbm = pl.BlockSpec(memory_space=pltpu.HBM)
    vmem = pl.BlockSpec(memory_space=pltpu.VMEM)
    smem = pl.BlockSpec(memory_space=pltpu.SMEM)
    return pl.pallas_call(
        functools.partial(main_kernel, capacity, span),
        out_shape=(
            jax.ShapeDtypeStruct((fields, cells_x * cells_y // 8 + 2 * PAD, lanes), f32),
            jax.ShapeDtypeStruct((per_dev,), jnp.int32),
        ),
        in_specs=[smem, smem, hbm, hbm, hbm, hbm, vmem, vmem],
        out_specs=(vmem, smem),
        scratch_shapes=[
            pltpu.VMEM((fields, cells_x + 2, cells_y + 16, lanes), f32),
            pltpu.VMEM((fields, cells_x, cells_y, lanes), f32),
            pltpu.VMEM((fields, cells_x, cells_y, lanes), f32),
            pltpu.VMEM((2, fields, cells_y, lanes), f32),
            pltpu.VMEM((2 * lanes, lanes), jnp.bfloat16),
            pltpu.SMEM((8, per_dev), jnp.int32),
            pltpu.SMEM((owners,), jnp.int32),
            pltpu.SemaphoreType.DMA((cells_x // PLANES, 3)),
            pltpu.SemaphoreType.DMA((1,)),
        ],
        compiler_params=pltpu.CompilerParams(vmem_limit_bytes=36 * MIB),
        cost_estimate=pl.CostEstimate(flops=100_000_000, bytes_accessed=27_700_000, transcendentals=0),
        name="residual_pool",
    )(myself, coupling, target, in_hbm(state), in_hbm(adjoint), in_hbm(source), kappa, flags)


def pack_kernel(tile_rows, slots, part, before, after, adjoint, flags, out, stage, pp, wv, pv, ev, gv, sems, tsem):
    fields, cells_y, lanes = before.shape
    cells_x = adjoint.shape[1]
    rows = cells_y // 4
    per_dev = slots.shape[0]
    cells = part.shape[1] - 2 * PAD
    span = cells // per_dev
    copies = []
    for i, x in enumerate((0, cells_x - 1)):
        copies.append(pltpu.make_async_copy(adjoint.at[:, x], ev.at[i], sems.at[i, 0]))
        copies.append(pltpu.make_async_copy(flags.at[x], gv.at[i], sems.at[i, 1]))
    for c in copies:
        c.start()
    pv[...] = pool_matrix(lanes)
    for f in range(fields):
        pp[f] = part[f]
    for c in copies:
        c.wait()
    for i, (face, at) in enumerate(((before, 0), (after, cells - rows))):
        for y in range(0, cells_y, 8):
            wgt = weight_of(gv[i, pl.ds(y, 8), :])
            for f in range(fields):
                wv[i, f, pl.ds(y, 8), :] = wgt * ev[i, f, pl.ds(y, 8), :] * face[f, pl.ds(y, 8), :]
        pooled = pooled_rows(wv.at[i], pv[...])
        for f in range(fields):
            pp[f, pl.ds(at + PAD, rows), :] = pp[f, pl.ds(at + PAD, rows), :] + pooled[f * rows : (f + 1) * rows]

    sub = lax.broadcasted_iota(jnp.int32, (8, lanes), 0)
    below = [None] + [sub < s for s in range(1, 8)]
    for t in range(per_dev):
        base = pl.multiple_of(slots[t] * tile_rows, 8)
        for v in range(tile_rows // 8):
            value = None
            for f in reversed(range(fields)):
                lo, hi = f * span - 8 * v, (f + 1) * span - 8 * v
                if hi <= 0 or lo >= 8:
                    continue
                piece = pp[f, pl.ds(PAD + span * t - lo, 8), :]
                value = piece if value is None else jnp.where(below[hi], piece, value)
            stage[pl.ds(t * tile_rows + 8 * v, 8), :] = value
        pltpu.make_async_copy(
            stage.at[pl.ds(t * tile_rows, tile_rows)], out.at[pl.ds(base, tile_rows)], tsem.at[0]
        ).start()
    pltpu.make_async_copy(stage, out.at[pl.ds(0, per_dev * tile_rows)], tsem.at[0]).wait()


def pack_part(part, slots, before, after, adjoint, flags, n_slots, tile_rows):
    fields, cells_x, cells_y, lanes = adjoint.shape
    f32 = jnp.float32
    vmem = pl.BlockSpec(memory_space=pltpu.VMEM)
    hbm = pl.BlockSpec(memory_space=pltpu.HBM)
    return pl.pallas_call(
        functools.partial(pack_kernel, tile_rows),
        out_shape=pltpu.HBM((n_slots * tile_rows, lanes), f32),
        in_specs=[pl.BlockSpec(memory_space=pltpu.SMEM), vmem, vmem, vmem, hbm, hbm],
        out_specs=hbm,
        scratch_shapes=[
            pltpu.VMEM((slots.shape[0] * tile_rows, lanes), f32),
            pltpu.VMEM(part.shape, f32),
            pltpu.VMEM((2, fields, cells_y, lanes), f32),
            pltpu.VMEM((2 * lanes, lanes), jnp.bfloat16),
            pltpu.VMEM((2, fields, cells_y, lanes), f32),
            pltpu.VMEM((2, cells_y, lanes), jnp.int32),
            pltpu.SemaphoreType.DMA((2, 2)),
            pltpu.SemaphoreType.DMA((1,)),
        ],
        compiler_params=pltpu.CompilerParams(vmem_limit_bytes=12 * MIB),
        cost_estimate=pl.CostEstimate(flops=1_000_000, bytes_accessed=3_500_000, transcendentals=0),
        name="edges_pack",
    )(slots, part, before, after, in_hbm(adjoint), in_hbm(flags))


def unpack_kernel(tile_rows, lookup, received, out, stage):
    fields, per_dev, width = out.shape
    lanes = received.shape[1]
    span = width // lanes

    for g in range(per_dev // 8):
        buf = stage.at[g % stage.shape[0]]
        for s in range(8):
            base = pl.multiple_of(lookup[g * 8 + s] * tile_rows, 8)
            buf[pl.ds(s * tile_rows, tile_rows), :] = received[pl.ds(base, tile_rows), :]
        for f in range(fields):
            for j in range(span):
                rows = buf[pl.ds(f * span + j, 8, stride=tile_rows), :]
                out[f, pl.ds(g * 8, 8), pl.ds(j * lanes, lanes)] = rows


def unpack_part(lookup, received, fields, per_dev, width, tile_rows):
    vmem = pl.BlockSpec(memory_space=pltpu.VMEM)
    lanes = received.shape[1]
    return pl.pallas_call(
        functools.partial(unpack_kernel, tile_rows),
        out_shape=jax.ShapeDtypeStruct((fields, per_dev, width), jnp.float32),
        in_specs=[pl.BlockSpec(memory_space=pltpu.SMEM), vmem],
        out_specs=vmem,
        scratch_shapes=[pltpu.VMEM((4, 8 * tile_rows, lanes), jnp.float32)],
        compiler_params=pltpu.CompilerParams(vmem_limit_bytes=8 * MIB),
        cost_estimate=pl.CostEstimate(flops=0, bytes_accessed=3_000_000, transcendentals=0),
        name="unpack",
    )(lookup, received)


def local(state, adjoint, source, kappa, cut_flags, coupling, target):
    state, adjoint, source, kappa, flags = (a[0] for a in (state, adjoint, source, kappa, cut_flags))
    fields, cells_x, cells_y, lanes = state.shape
    groups, bricks = lax.axis_size("grp"), lax.axis_size("brk")
    owners = groups * bricks
    per_dev = target.shape[1]
    capacity = per_dev // ((groups - 1) * bricks) + 1
    width = cells_x * cells_y * lanes // 8 // per_dev
    span = width // lanes
    tile_rows = -(-span * fields // 8) * 8
    myself = lax.axis_index(("grp", "brk"))

    up = [(i, i + 1) for i in range(bricks - 1)]
    down = [(j, i) for i, j in up]
    first, last = faces_of(state)
    before = lax.ppermute(last, "brk", up)
    after = lax.ppermute(first, "brk", down)

    part, slots = main_part(
        state, adjoint, source, kappa, flags, coupling, target, myself.reshape(1), capacity, span
    )
    outgoing = pack_part(part, slots, before, after, adjoint, flags, owners * capacity, tile_rows)
    outgoing = outgoing.reshape(owners, capacity * tile_rows, lanes)
    incoming = lax.all_to_all(outgoing, ("grp", "brk"), 0, 0, tiled=True)
    incoming = incoming.reshape(owners * capacity * tile_rows, lanes)

    slot_ids = myself * per_dev + jnp.arange(per_dev, dtype=jnp.int32)
    codes = jnp.arange(owners * per_dev, dtype=jnp.int32)
    hit = target.reshape(-1)[None, :] == slot_ids[:, None]
    origin = jnp.sum(jnp.where(hit, codes[None, :], 0), axis=1)
    sender = origin // per_dev
    before_it = jnp.logical_and(sender[:, None] == sender[None, :], origin[None, :] < origin[:, None])
    lookup = sender * capacity + jnp.sum(before_it.astype(jnp.int32), axis=1)
    out = unpack_part(lookup, incoming, fields, per_dev, width, tile_rows)
    return out.transpose(1, 0, 2)


def solution(mesh):
    placed = (
        P("grp", None, "brk", None, None),
        P("grp", None, "brk", None, None),
        P("grp", None, "brk", None, None),
        P("grp", "brk", None, None),
        P("grp", "brk", None, None),
        P(),
        P(),
    )
    return jax.shard_map(
        local, mesh=mesh, in_specs=placed, out_specs=P(("grp", "brk"), None, None), check_vma=False
    )
```

time: 83.3 us -> 64.5 us (0.77)
  local copies, waits for them, and re-layouts: 10 us -> 0.02 us
  Pallas kernels: 23.2 us -> 16.4 us
  starting transfers between devices: 19.2 us -> 17.4 us
    pallas_call x3 -> x4, Pallas kernels: 23.2 us -> 16.4 us  [the longest x1 9.76 us: main_part(): pl.pallas_call(functools.partial(main_kernel, capacity, span), out_shape=...]
    unnamed x7 -> x8, local copies, waits for them, and re-layouts: 5.34 us -> 0.02 us
    all_to_all x2 -> x0, local copies, waits for them, and re-layouts: 4.09 us -> none  [local(): incoming = lax.all_to_all(outgoing, ('grp', 'brk'), 0, 0, tiled=True)]
    all_to_all x1, starting transfers between devices: 13.3 us -> 12.1 us  [local(): incoming = lax.all_to_all(outgoing, ('grp', 'brk'), 0, 0, tiled=True)]
  transfers between devices with their start and end apart: 3 -> 3, of which waited for: 1 -> 1; matrix products, arithmetic and copies ran while one was open for 3% -> 2% of each run, Pallas kernels for 17% -> 15%
where the time goes in v2:
time: 64.5 us; the launch traced here: 64.3 us
  waiting for transfers between devices  28.9 us (45%)
  starting transfers between devices  17.4 us (27%)
  Pallas kernels  16.4 us (25%)
  other arithmetic  1.53 us (2%)
    all_to_all x1, waiting for transfers between devices, local(): incoming = lax.all_to_all(outgoing, ('grp', 'brk'), 0, 0, tiled=True)  28.9 us
    all_to_all x1, starting transfers between devices, local(): incoming = lax.all_to_all(outgoing, ('grp', 'brk'), 0, 0, tiled=True)  12.1 us
    pallas_call x1, Pallas kernels, main_part(): pl.pallas_call(functools.partial(main_kernel, capacity, span), out_shape=...  9.76 us
    ppermute x1, starting transfers between devices, local(): before = lax.ppermute(last, 'brk', up)  3.95 us
    pallas_call x1, Pallas kernels, pack_part(): pl.pallas_call(functools.partial(pack_kernel, tile_rows), out_shape=pltpu...  2.87 us
    pallas_call x1, Pallas kernels, faces_of(): pl.pallas_call(face_kernel, out_shape=(face, face), in_specs=[pl.BlockSpe...  1.87 us
    pallas_call x1, Pallas kernels, unpack_part(): pl.pallas_call(functools.partial(unpack_kernel, tile_rows), out_shape=jax...  1.87 us
    reduce_sum x1, other arithmetic, local(): origin = jnp.sum(jnp.where(hit, codes[None, :], 0), axis=1)  1.32 us
  transfers between devices with their start and end apart: 3, of which 1 were waited for; matrix products, arithmetic and copies ran while one was open for 2% of the time, Pallas kernels for 15%

profile of v2, /device:TPU:1, one launch (start us, length us, event | category | flops | bytes accessed | tf_op | source)
XLA Modules:
  0.0 64.3 jit_solution(634426478816922476)
XLA Ops:
  0.0 0.0 copy-start.2
  0.0 0.0 copy-start.3
  0.0 0.0 copy-start
  0.0 0.0 copy-start.1
  0.0 1.9 %faces.1 = (f32[5,64,128]{2,1,0:T(8,128)}, f32[5,64,128]{2,1,0:T(8,128)}) custom-call(f32[5,48,64,128]{3,2,1,0:T(8,128)} %bitcast.15), custom_call_target="tpu_custom_call" | custom-call | bytes 650000 | tf_op jit(solution)/shard_map/faces/pallas_call | solution.py:57
  1.9 4.0 %collective-permute-start = (f32[5,64,128]{2,1,0:T(8,128)}, f32[5,64,128]{2,1,0:T(8,128)S(1)}, u32[]{:S(2)}, u32[]{:S(2)}) collective-permute-start(f32[5,64,128]{2,1,0:T(8,128)} %get-tuple-element.11), channel_id=1, source_target_pairs={{0,1},{1,2},{2,3},{3,4},{4,5},{5,6},{6,7},{8,9},{9,10},{10,11},{11... | collective-permute-start | bytes 491528 | tf_op jit(solution)/shard_map/ppermute | solution.py:329
  5.9 1.3 %collective-permute-start.1 = (f32[5,64,128]{2,1,0:T(8,128)}, f32[5,64,128]{2,1,0:T(8,128)S(1)}, u32[]{:S(2)}, u32[]{:S(2)}) collective-permute-start(f32[5,64,128]{2,1,0:T(8,128)} %get-tuple-element.12), channel_id=1, source_target_pairs={{1,0},{2,1},{3,2},{4,3},{5,4},{6,5},{7,6},{9,8},{10,9},{11,10},{12... | collective-permute-start | bytes 491528 | tf_op jit(solution)/shard_map/ppermute | solution.py:330
  7.2 0.0 copy-done.2
  7.2 0.0 copy-done.3
  7.2 0.0 copy-done
  7.2 0.0 copy-done.1
  7.2 9.8 %residual_pool.1 = (f32[5,400,128]{2,1,0:T(8,128)S(1)}, s32[128]{0:T(128)S(1)}) custom-call(s32[1]{0:T(128)} %bitcast.1.myself, f32[5,5]{1,0:T(8,128)S(1)} %copy-done.3, s32[128,128]{1,0:T(8,128)S(1)} %copy-done.2, f32[5,48,64,128]{3,2,1,0:T(8,128)} %bitcast.16, f32[5,48,64,128]{3,2,1,0:T(8,128)} %bitcast.17, f32[5,48,64,128]{3,2,1,0:T(8,128)} %bitcast.20, ...), custom_call_target="tpu_custom_call" | custom-call | flops 100000000 | bytes 27700000 | tf_op jit(solution)/shard_map/residual_pool/pallas_call | solution.py:186
  17.0 0.0 collective-permute-done.before
  17.0 0.0 collective-permute-done.1.after
  17.0 2.9 %edges_pack.1 = f32[4096,128]{1,0:T(8,128)} custom-call(s32[128]{0:T(128)S(1)} %get-tuple-element.9.slots, f32[5,400,128]{2,1,0:T(8,128)S(1)} %get-tuple-element.10.part, f32[5,64,128]{2,1,0:T(8,128)S(1)} %collective-permute-done.before, f32[5,64,128]{2,1,0:T(8,128)S(1)} %collective-permute-done.1.after, f32[5,48,64,128]{3,2,1,0:T(8,128)} %bitcast.18, ...), custom_call_target="tpu_custom_call" | custom-call | flops 1000000 | bytes 3500000 | tf_op jit(solution)/shard_map/edges_pack/pallas_call | solution.py:262
  19.9 12.1 %all-to-all-start = ((f32[128,32,128]{2,1,0:T(8,128)}), f32[128,32,128]{2,1,0:T(8,128)S(1)}, u32[]{:S(2)}, u32[]{:S(2)}) async-start(f32[128,32,128]{2,1,0:T(8,128)} %bitcast.19), calls=%async_computation | async-start | bytes 4194304 | tf_op jit(solution)/shard_map/all_to_all | solution.py:337
  32.0 1.3 %select_reduce_fusion = s32[128]{0:T(128)S(1)} fusion(s32[16384]{0:T(1024)S(1)} %bitcast.14, s32[128]{0:T(128)S(1)} %iota_add_fusion), kind=kLoop, calls=%fused_computation | loop fusion | flops 6291328 | bytes 66560 | tf_op jit(solution)/shard_map/reduce_sum | solution.py:343
  33.3 0.2 convert_reduce_fusion
  33.5 28.9 %all-to-all-done = f32[128,32,128]{2,1,0:T(8,128)S(1)} async-done(((f32[128,32,128]{2,1,0:T(8,128)}), f32[128,32,128]{2,1,0:T(8,128)S(1)}, u32[]{:S(2)}, u32[]{:S(2)}) %all-to-all-start) | async-done | bytes 2097184 | tf_op jit(solution)/shard_map/all_to_all | solution.py:337
  62.4 1.9 %unpack.1 = f32[5,128,384]{2,1,0:T(8,128)} custom-call(s32[128]{0:T(128)S(1)} %multiply_add_fusion.lookup, f32[4096,128]{1,0:T(8,128)S(1)} %bitcast.10), custom_call_target="tpu_custom_call" | custom-call | bytes 3000000 | tf_op jit(solution)/shard_map/unpack/pallas_call | solution.py:302
  (3 shorter events, 0.0 us)
Async XLA Ops:
  0.0 7.2 %copy-start.2 = (s32[128,128]{1,0:T(8,128)S(1)}, s32[128,128]{1,0:T(8,128)}, u32[]{:S(2)}) copy-start(s32[128,128]{1,0:T(8,128)} %target.1) | copy-start | bytes 196612
  0.0 7.2 %copy-start.3 = (f32[5,5]{1,0:T(8,128)S(1)}, f32[5,5]{1,0:T(8,128)}, u32[]{:S(2)}) copy-start(f32[5,5]{1,0:T(8,128)} %coupling.1) | copy-start | bytes 304
  0.0 7.2 %copy-start = (s32[1,48,64,128]{3,2,1,0:T(8,128)S(1)}, s32[1,48,64,128]{3,2,1,0:T(8,128)}, u32[]{:S(2)}) copy-start(s32[1,48,64,128]{3,2,1,0:T(8,128)} %param.11) | copy-start | bytes 4718596
  0.0 7.2 %copy-start.1 = (f32[1,48,64,128]{3,2,1,0:T(8,128)S(1)}, f32[1,48,64,128]{3,2,1,0:T(8,128)}, u32[]{:S(2)}) copy-start(f32[1,48,64,128]{3,2,1,0:T(8,128)} %param.10) | copy-start | bytes 4718596
  1.9 15.1 %collective-permute-start = (f32[5,64,128]{2,1,0:T(8,128)}, f32[5,64,128]{2,1,0:T(8,128)S(1)}, u32[]{:S(2)}, u32[]{:S(2)}) collective-permute-start(f32[5,64,128]{2,1,0:T(8,128)} %get-tuple-element.11), channel_id=1, source_target_pairs={{0,1},{1,2},{2,3},{3,4},{4,5},{5,6},{6,7},{8,9},{9,10},{10,11},{11... | collective-permute-start | bytes 491528 | tf_op jit(solution)/shard_map/ppermute | solution.py:329
  5.9 11.1 %collective-permute-start.1 = (f32[5,64,128]{2,1,0:T(8,128)}, f32[5,64,128]{2,1,0:T(8,128)S(1)}, u32[]{:S(2)}, u32[]{:S(2)}) collective-permute-start(f32[5,64,128]{2,1,0:T(8,128)} %get-tuple-element.12), channel_id=1, source_target_pairs={{1,0},{2,1},{3,2},{4,3},{5,4},{6,5},{7,6},{9,8},{10,9},{11,10},{12... | collective-permute-start | bytes 491528 | tf_op jit(solution)/shard_map/ppermute | solution.py:330
  19.9 42.5 %all-to-all-start = ((f32[128,32,128]{2,1,0:T(8,128)}), f32[128,32,128]{2,1,0:T(8,128)S(1)}, u32[]{:S(2)}, u32[]{:S(2)}) async-start(f32[128,32,128]{2,1,0:T(8,128)} %bitcast.19), calls=%async_computation | async-start | bytes 4194304 | tf_op jit(solution)/shard_map/all_to_all | solution.py:337

commit v3 on v2

--- a/solution.py
+++ b/solution.py
@@ -40,6 +40,38 @@
     return dot(first, matrix) + dot(second, matrix)
 
 
+def tile_values(load, fields, span, tile_rows, lanes):
+    sub = lax.broadcasted_iota(jnp.int32, (8, lanes), 0)
+    values = []
+    for v in range(tile_rows // 8):
+        value = None
+        for f in reversed(range(fields)):
+            lo, hi = f * span - 8 * v, (f + 1) * span - 8 * v
+            if hi <= 0 or lo >= 8:
+                continue
+            piece = load(f, -lo)
+            value = piece if value is None else jnp.where(sub < hi, piece, value)
+        values.append(value)
+    return values
+
+
+def send_tile(slot, at, values, stage, out, tile_rows, sem):
+    for v, value in enumerate(values):
+        stage[pl.ds(pl.multiple_of(at * tile_rows + 8 * v, 8), 8), :] = value
+    here = pl.ds(pl.multiple_of(at * tile_rows, 8), tile_rows)
+    there = pl.ds(pl.multiple_of(slot * tile_rows, 8), tile_rows)
+    pltpu.make_async_copy(stage.at[here], out.at[there], sem).start()
+
+
+def await_tiles(first, count, stage, out, tile_rows, sem):
+    rows = count * tile_rows
+    pltpu.make_async_copy(stage.at[pl.ds(first * tile_rows, rows)], out.at[pl.ds(0, rows)], sem).wait()
+
+
+def edge_tiles(rows, span):
+    return -(-rows // span)
+
+
 def face_kernel(state, first, last, sems):
     cells_x = state.shape[1]
     one = pltpu.make_async_copy(state.at[:, 0], first, sems.at[0])
@@ -52,13 +84,13 @@
 
 def faces_of(state):
     fields, _, cells_y, lanes = state.shape
-    face = jax.ShapeDtypeStruct((fields, cells_y, lanes), jnp.float32)
-    vmem = pl.BlockSpec(memory_space=pltpu.VMEM)
+    face = pltpu.HBM((fields, cells_y, lanes), jnp.float32)
+    hbm = pl.BlockSpec(memory_space=pltpu.HBM)
     return pl.pallas_call(
         face_kernel,
         out_shape=(face, face),
-        in_specs=[pl.BlockSpec(memory_space=pltpu.HBM)],
-        out_specs=(vmem, vmem),
+        in_specs=[hbm],
+        out_specs=(hbm, hbm),
         scratch_shapes=[pltpu.SemaphoreType.DMA((2,))],
         compiler_params=pltpu.CompilerParams(vmem_limit_bytes=2 * MIB),
         cost_estimate=pl.CostEstimate(flops=0, bytes_accessed=650_000, transcendentals=0),
@@ -67,8 +99,8 @@
 
 
 def main_kernel(
-    capacity, span, myself, coupling, target, state, adjoint, source, kv, fv,
-    out, slots, sv, av, bv, wv, pv, tv, seen, sems, tsem,
+    capacity, span, tile_rows, myself, coupling, target, state, adjoint, source, kv, fv,
+    sent, slots, ends, duals, out, stage, sv, av, bv, wv, pv, tv, seen, sems, tsem,
 ):
     fields, cells_x, cells_y, lanes = adjoint.shape
     steps = cells_x // PLANES
@@ -133,8 +165,22 @@
             out[f, pl.ds(pl.multiple_of(at + PAD, 8), rows), :] = pooled[f * rows : (f + 1) * rows]
 
     copy(0, 0).wait()
+    edge = edge_tiles(rows, span)
+    batch = PLANES // 2 * rows // span
+
+    def place(first, count):
+        for i in range(count):
+            t = first + i
+            values = tile_values(
+                lambda f, d: out[f, pl.ds(PAD + span * t + d, 8), :], fields, span, tile_rows, lanes
+            )
+            send_tile(slots[t], t, values, stage, sent, tile_rows, tsem.at[1])
 
     def step_body(step, carry):
+        @pl.when(step >= 2)
+        def _():
+            place(edge + batch * (step - 2), batch)
+
         @pl.when(step + AHEAD < steps)
         def _():
             start(step + AHEAD)
@@ -174,24 +220,41 @@
 
     lax.fori_loop(0, steps, step_body, 0)
     pool(1, (cells_x // 2 - 1) * rows)
-
-
-def main_part(state, adjoint, source, kappa, flags, coupling, target, myself, capacity, span):
+    done = edge + batch * (steps - 2)
+    place(done, per_dev - edge - done)
+    for i, x in enumerate((0, cells_x - 1)):
+        for y in range(0, cells_y, 8):
+            wgt = weight_of(fv[x, pl.ds(y, 8), :])
+            for f in range(fields):
+                duals[i, f, pl.ds(y, 8), :] = wgt * av[f, x, pl.ds(y, 8), :]
+    kept = ends.shape[2]
+    for f in range(fields):
+        ends[0, f] = out[f, pl.ds(PAD, kept), :]
+        ends[1, f] = out[f, pl.ds(PAD + per_dev * span - kept, kept), :]
+    await_tiles(edge, per_dev - 2 * edge, stage, sent, tile_rows, tsem.at[1])
+
+
+def main_part(state, adjoint, source, kappa, flags, coupling, target, myself, capacity, span, tile_rows):
     fields, cells_x, cells_y, lanes = state.shape
     owners, per_dev = target.shape
+    kept = -(-edge_tiles(cells_y // 4, span) * span // 8) * 8
     f32 = jnp.float32
     hbm = pl.BlockSpec(memory_space=pltpu.HBM)
     vmem = pl.BlockSpec(memory_space=pltpu.VMEM)
     smem = pl.BlockSpec(memory_space=pltpu.SMEM)
     return pl.pallas_call(
-        functools.partial(main_kernel, capacity, span),
+        functools.partial(main_kernel, capacity, span, tile_rows),
         out_shape=(
-            jax.ShapeDtypeStruct((fields, cells_x * cells_y // 8 + 2 * PAD, lanes), f32),
+            pltpu.HBM((owners * capacity * tile_rows, lanes), f32),
             jax.ShapeDtypeStruct((per_dev,), jnp.int32),
+            pltpu.VMEM((2, fields, kept, lanes), f32),
+            pltpu.VMEM((2, fields, cells_y, lanes), f32),
         ),
         in_specs=[smem, smem, hbm, hbm, hbm, hbm, vmem, vmem],
-        out_specs=(vmem, smem),
+        out_specs=(hbm, smem, vmem, vmem),
         scratch_shapes=[
+            pltpu.VMEM((fields, per_dev * span + 2 * PAD, lanes), f32),
+            pltpu.VMEM((per_dev * tile_rows, lanes), f32),
             pltpu.VMEM((fields, cells_x + 2, cells_y + 16, lanes), f32),
             pltpu.VMEM((fields, cells_x, cells_y, lanes), f32),
             pltpu.VMEM((fields, cells_x, cells_y, lanes), f32),
@@ -200,7 +263,7 @@
             pltpu.SMEM((8, per_dev), jnp.int32),
             pltpu.SMEM((owners,), jnp.int32),
             pltpu.SemaphoreType.DMA((cells_x // PLANES, 3)),
-            pltpu.SemaphoreType.DMA((1,)),
+            pltpu.SemaphoreType.DMA((2,)),
         ],
         compiler_params=pltpu.CompilerParams(vmem_limit_bytes=36 * MIB),
         cost_estimate=pl.CostEstimate(flops=100_000_000, bytes_accessed=27_700_000, transcendentals=0),
@@ -208,82 +271,65 @@
     )(myself, coupling, target, in_hbm(state), in_hbm(adjoint), in_hbm(source), kappa, flags)
 
 
-def pack_kernel(tile_rows, slots, part, before, after, adjoint, flags, out, stage, pp, wv, pv, ev, gv, sems, tsem):
+def edge_kernel(span, tile_rows, slots, ends, duals, before, after, sent, out, stage, pe, wv, pv, sem):
     fields, cells_y, lanes = before.shape
-    cells_x = adjoint.shape[1]
     rows = cells_y // 4
     per_dev = slots.shape[0]
-    cells = part.shape[1] - 2 * PAD
-    span = cells // per_dev
-    copies = []
-    for i, x in enumerate((0, cells_x - 1)):
-        copies.append(pltpu.make_async_copy(adjoint.at[:, x], ev.at[i], sems.at[i, 0]))
-        copies.append(pltpu.make_async_copy(flags.at[x], gv.at[i], sems.at[i, 1]))
-    for c in copies:
-        c.start()
+    kept = ends.shape[2]
+    edge = edge_tiles(rows, span)
     pv[...] = pool_matrix(lanes)
-    for f in range(fields):
-        pp[f] = part[f]
-    for c in copies:
-        c.wait()
-    for i, (face, at) in enumerate(((before, 0), (after, cells - rows))):
+    for i, (face, at) in enumerate(((before, 0), (after, kept - rows))):
         for y in range(0, cells_y, 8):
-            wgt = weight_of(gv[i, pl.ds(y, 8), :])
             for f in range(fields):
-                wv[i, f, pl.ds(y, 8), :] = wgt * ev[i, f, pl.ds(y, 8), :] * face[f, pl.ds(y, 8), :]
+                wv[i, f, pl.ds(y, 8), :] = duals[i, f, pl.ds(y, 8), :] * face[f, pl.ds(y, 8), :]
         pooled = pooled_rows(wv.at[i], pv[...])
         for f in range(fields):
-            pp[f, pl.ds(at + PAD, rows), :] = pp[f, pl.ds(at + PAD, rows), :] + pooled[f * rows : (f + 1) * rows]
-
-    sub = lax.broadcasted_iota(jnp.int32, (8, lanes), 0)
-    below = [None] + [sub < s for s in range(1, 8)]
-    for t in range(per_dev):
-        base = pl.multiple_of(slots[t] * tile_rows, 8)
-        for v in range(tile_rows // 8):
-            value = None
-            for f in reversed(range(fields)):
-                lo, hi = f * span - 8 * v, (f + 1) * span - 8 * v
-                if hi <= 0 or lo >= 8:
-                    continue
-                piece = pp[f, pl.ds(PAD + span * t - lo, 8), :]
-                value = piece if value is None else jnp.where(below[hi], piece, value)
-            stage[pl.ds(t * tile_rows + 8 * v, 8), :] = value
-        pltpu.make_async_copy(
-            stage.at[pl.ds(t * tile_rows, tile_rows)], out.at[pl.ds(base, tile_rows)], tsem.at[0]
-        ).start()
-    pltpu.make_async_copy(stage, out.at[pl.ds(0, per_dev * tile_rows)], tsem.at[0]).wait()
-
-
-def pack_part(part, slots, before, after, adjoint, flags, n_slots, tile_rows):
-    fields, cells_x, cells_y, lanes = adjoint.shape
+            pe[i, f, pl.ds(PAD, kept), :] = ends[i, f]
+            here = pl.ds(at + PAD, rows)
+            pe[i, f, here, :] = pe[i, f, here, :] + pooled[f * rows : (f + 1) * rows]
+    for i, (tile, start) in enumerate(((0, 0), (per_dev - edge, kept - edge * span))):
+        for k in range(edge):
+            values = tile_values(
+                lambda f, d: pe[i, f, pl.ds(PAD + start + span * k + d, 8), :], fields, span, tile_rows, lanes
+            )
+            send_tile(slots[tile + k], i * edge + k, values, stage, out, tile_rows, sem.at[0])
+    await_tiles(0, 2 * edge, stage, out, tile_rows, sem.at[0])
+
+
+def edge_part(sent, slots, ends, duals, before, after, span, tile_rows):
+    fields, cells_y, lanes = before.shape
     f32 = jnp.float32
     vmem = pl.BlockSpec(memory_space=pltpu.VMEM)
     hbm = pl.BlockSpec(memory_space=pltpu.HBM)
+    edge = edge_tiles(cells_y // 4, span)
     return pl.pallas_call(
-        functools.partial(pack_kernel, tile_rows),
-        out_shape=pltpu.HBM((n_slots * tile_rows, lanes), f32),
-        in_specs=[pl.BlockSpec(memory_space=pltpu.SMEM), vmem, vmem, vmem, hbm, hbm],
+        functools.partial(edge_kernel, span, tile_rows),
+        out_shape=pltpu.HBM(sent.shape, f32),
+        in_specs=[pl.BlockSpec(memory_space=pltpu.SMEM), vmem, vmem, vmem, vmem, hbm],
         out_specs=hbm,
         scratch_shapes=[
-            pltpu.VMEM((slots.shape[0] * tile_rows, lanes), f32),
-            pltpu.VMEM(part.shape, f32),
+            pltpu.VMEM((2 * edge * tile_rows, lanes), f32),
+            pltpu.VMEM((2, fields, ends.shape[2] + 2 * PAD, lanes), f32),
             pltpu.VMEM((2, fields, cells_y, lanes), f32),
             pltpu.VMEM((2 * lanes, lanes), jnp.bfloat16),
-            pltpu.VMEM((2, fields, cells_y, lanes), f32),
-            pltpu.VMEM((2, cells_y, lanes), jnp.int32),
-            pltpu.SemaphoreType.DMA((2, 2)),
             pltpu.SemaphoreType.DMA((1,)),
         ],
+        input_output_aliases={5: 0},
         compiler_params=pltpu.CompilerParams(vmem_limit_bytes=12 * MIB),
-        cost_estimate=pl.CostEstimate(flops=1_000_000, bytes_accessed=3_500_000, transcendentals=0),
-        name="edges_pack",
-    )(slots, part, before, after, in_hbm(adjoint), in_hbm(flags))
-
-
-def unpack_kernel(tile_rows, lookup, received, out, stage):
-    fields, per_dev, width = out.shape
+        cost_estimate=pl.CostEstimate(flops=1_000_000, bytes_accessed=100_000, transcendentals=0),
+        name="edges",
+    )(slots, ends, duals, before, after, in_hbm(sent))
+
+
+def unpack_kernel(tile_rows, lookup, received, out, stage, built, sems):
+    fields, per_dev, width = built.shape
     lanes = received.shape[1]
     span = width // lanes
+    piece = per_dev // sems.shape[0]
+
+    def leave(k):
+        here = pl.ds(k * piece, piece)
+        return pltpu.make_async_copy(built.at[:, here], out.at[:, here], sems.at[k])
 
     for g in range(per_dev // 8):
         buf = stage.at[g % stage.shape[0]]
@@ -293,18 +339,25 @@
         for f in range(fields):
             for j in range(span):
                 rows = buf[pl.ds(f * span + j, 8, stride=tile_rows), :]
-                out[f, pl.ds(g * 8, 8), pl.ds(j * lanes, lanes)] = rows
+                built[f, pl.ds(g * 8, 8), pl.ds(j * lanes, lanes)] = rows
+        if (g + 1) * 8 % piece == 0:
+            leave(g * 8 // piece).start()
+    for k in range(sems.shape[0]):
+        leave(k).wait()
 
 
 def unpack_part(lookup, received, fields, per_dev, width, tile_rows):
-    vmem = pl.BlockSpec(memory_space=pltpu.VMEM)
     lanes = received.shape[1]
     return pl.pallas_call(
         functools.partial(unpack_kernel, tile_rows),
         out_shape=jax.ShapeDtypeStruct((fields, per_dev, width), jnp.float32),
-        in_specs=[pl.BlockSpec(memory_space=pltpu.SMEM), vmem],
-        out_specs=vmem,
-        scratch_shapes=[pltpu.VMEM((4, 8 * tile_rows, lanes), jnp.float32)],
+        in_specs=[pl.BlockSpec(memory_space=pltpu.SMEM), pl.BlockSpec(memory_space=pltpu.VMEM)],
+        out_specs=pl.BlockSpec(memory_space=pltpu.HBM),
+        scratch_shapes=[
+            pltpu.VMEM((4, 8 * tile_rows, lanes), jnp.float32),
+            pltpu.VMEM((fields, per_dev, width), jnp.float32),
+            pltpu.SemaphoreType.DMA((4,)),
+        ],
         compiler_params=pltpu.CompilerParams(vmem_limit_bytes=8 * MIB),
         cost_estimate=pl.CostEstimate(flops=0, bytes_accessed=3_000_000, transcendentals=0),
         name="unpack",
@@ -329,10 +382,10 @@
     before = lax.ppermute(last, "brk", up)
     after = lax.ppermute(first, "brk", down)
 
-    part, slots = main_part(
-        state, adjoint, source, kappa, flags, coupling, target, myself.reshape(1), capacity, span
+    sent, slots, ends, duals = main_part(
+        state, adjoint, source, kappa, flags, coupling, target, myself.reshape(1), capacity, span, tile_rows
     )
-    outgoing = pack_part(part, slots, before, after, adjoint, flags, owners * capacity, tile_rows)
+    outgoing = edge_part(sent, slots, ends, duals, before, after, span, tile_rows)
     outgoing = outgoing.reshape(owners, capacity * tile_rows, lanes)
     incoming = lax.all_to_all(outgoing, ("grp", "brk"), 0, 0, tiled=True)
     incoming = incoming.reshape(owners * capacity * tile_rows, lanes)

time: 64.5 us -> 74.6 us (1.16)
  Pallas kernels: 16.4 us -> 26.5 us
    pallas_call x3, Pallas kernels: 14.5 us -> 24.9 us  [the longest x1 12.4 us: main_part(): pl.pallas_call(functools.partial(main_kernel, capacity, span, tile_rows),...]
  transfers between devices with their start and end apart: 3 -> 3, of which waited for: 1 -> 1; matrix products, arithmetic and copies ran while one was open for 2% -> 2% of each run, Pallas kernels for 15% -> 17%
where the time goes in v3:
time: 74.6 us; the launch traced here: 74.4 us
  waiting for transfers between devices  28.9 us (39%)
  Pallas kernels  26.5 us (36%)
  starting transfers between devices  17.4 us (23%)
  other arithmetic  1.53 us (2%)
    all_to_all x1, waiting for transfers between devices, local(): incoming = lax.all_to_all(outgoing, ('grp', 'brk'), 0, 0, tiled=True)  28.9 us
    pallas_call x1, Pallas kernels, main_part(): pl.pallas_call(functools.partial(main_kernel, capacity, span, tile_rows),...  12.4 us
    all_to_all x1, starting transfers between devices, local(): incoming = lax.all_to_all(outgoing, ('grp', 'brk'), 0, 0, tiled=True)  12.1 us
    pallas_call x1, Pallas kernels, faces_of(): pl.pallas_call(face_kernel, out_shape=(face, face), in_specs=[hbm], out_s...  11 us
    ppermute x1, starting transfers between devices, local(): before = lax.ppermute(last, 'brk', up)  3.95 us
    pallas_call x1, Pallas kernels, unpack_part(): pl.pallas_call(functools.partial(unpack_kernel, tile_rows), out_shape=jax...  1.65 us
  transfers between devices with their start and end apart: 3, of which 1 were waited for; matrix products, arithmetic and copies ran while one was open for 2% of the time, Pallas kernels for 17%

profile of v3, /device:TPU:1, one launch (start us, length us, event | category | flops | bytes accessed | tf_op | source)
XLA Modules:
  0.0 74.4 jit_solution(13632660018617682068)
XLA Ops:
  0.0 0.0 copy-start.2
  0.0 0.0 copy-start.3
  0.0 0.0 copy-start.1
  0.0 0.0 copy-start
  0.0 11.0 %faces.1 = (f32[5,64,128]{2,1,0:T(8,128)}, f32[5,64,128]{2,1,0:T(8,128)}) custom-call(f32[5,48,64,128]{3,2,1,0:T(8,128)} %bitcast.14), custom_call_target="tpu_custom_call" | custom-call | bytes 650000 | tf_op jit(solution)/shard_map/faces/pallas_call | solution.py:89
  11.1 4.0 %collective-permute-start = (f32[5,64,128]{2,1,0:T(8,128)}, f32[5,64,128]{2,1,0:T(8,128)S(1)}, u32[]{:S(2)}, u32[]{:S(2)}) collective-permute-start(f32[5,64,128]{2,1,0:T(8,128)} %get-tuple-element.14), channel_id=1, source_target_pairs={{0,1},{1,2},{2,3},{3,4},{4,5},{5,6},{6,7},{8,9},{9,10},{10,11},{11... | collective-permute-start | bytes 491528 | tf_op jit(solution)/shard_map/ppermute | solution.py:382
  15.0 1.3 %collective-permute-start.1 = (f32[5,64,128]{2,1,0:T(8,128)}, f32[5,64,128]{2,1,0:T(8,128)S(1)}, u32[]{:S(2)}, u32[]{:S(2)}) collective-permute-start(f32[5,64,128]{2,1,0:T(8,128)} %get-tuple-element.15), channel_id=1, source_target_pairs={{1,0},{2,1},{3,2},{4,3},{5,4},{6,5},{7,6},{9,8},{10,9},{11,10},{12... | collective-permute-start | bytes 491528 | tf_op jit(solution)/shard_map/ppermute | solution.py:383
  16.3 0.0 copy-done.2
  16.4 0.0 copy-done.3
  16.4 0.0 copy-done.1
  16.4 0.0 copy-done
  16.4 12.4 %residual_pool.1 = (f32[4096,128]{1,0:T(8,128)}, s32[128]{0:T(128)S(1)}, f32[2,5,24,128]{3,2,1,0:T(8,128)S(1)}, f32[2,5,64,128]{3,2,1,0:T(8,128)S(1)}) custom-call(s32[1]{0:T(128)} %bitcast.1.myself, f32[5,5]{1,0:T(8,128)S(1)} %copy-done.3, s32[128,128]{1,0:T(8,128)S(1)} %copy-done.2, f32[5,48,64,128]{3,2,1,0:T(8,128)} %bitcast.15, ...), custom_call_target="tpu_custom_call" | custom-call | flops 100000000 | bytes 27700000 | tf_op jit(solution)/shard_map/residual_pool/pallas_call | solution.py:245
  28.8 0.0 collective-permute-done.before
  28.8 0.0 collective-permute-done.1.after
  28.8 1.4 %edges.1 = f32[4096,128]{1,0:T(8,128)} custom-call(s32[128]{0:T(128)S(1)} %get-tuple-element.11.slots, f32[2,5,24,128]{3,2,1,0:T(8,128)S(1)} %get-tuple-element.12.ends, f32[2,5,64,128]{3,2,1,0:T(8,128)S(1)} %get-tuple-element.13.duals, f32[5,64,128]{2,1,0:T(8,128)S(1)} %collective-permute-done.before, ...), custom_call_target="tpu_custom_call", output_to_operand_aliasing={{}: (5, {})} | custom-call | flops 1000000 | bytes 100000 | tf_op jit(solution)/shard_map/edges/pallas_call | solution.py:305
  30.2 12.1 %all-to-all-start = ((f32[128,32,128]{2,1,0:T(8,128)}), f32[128,32,128]{2,1,0:T(8,128)S(1)}, u32[]{:S(2)}, u32[]{:S(2)}) async-start(f32[128,32,128]{2,1,0:T(8,128)} %bitcast.16), calls=%async_computation | async-start | bytes 4194304 | tf_op jit(solution)/shard_map/all_to_all | solution.py:390
  42.4 1.3 %select_reduce_fusion = s32[128]{0:T(128)S(1)} fusion(s32[16384]{0:T(1024)S(1)} %bitcast.13, s32[128]{0:T(128)S(1)} %iota_add_fusion), kind=kLoop, calls=%fused_computation | loop fusion | flops 6291328 | bytes 66560 | tf_op jit(solution)/shard_map/reduce_sum | solution.py:396
  43.7 0.2 convert_reduce_fusion
  43.9 28.9 %all-to-all-done = f32[128,32,128]{2,1,0:T(8,128)S(1)} async-done(((f32[128,32,128]{2,1,0:T(8,128)}), f32[128,32,128]{2,1,0:T(8,128)S(1)}, u32[]{:S(2)}, u32[]{:S(2)}) %all-to-all-start) | async-done | bytes 2097184 | tf_op jit(solution)/shard_map/all_to_all | solution.py:390
  72.7 1.6 %unpack.1 = f32[5,128,384]{2,1,0:T(8,128)} custom-call(s32[128]{0:T(128)S(1)} %multiply_add_fusion.lookup, f32[4096,128]{1,0:T(8,128)S(1)} %bitcast.10), custom_call_target="tpu_custom_call" | custom-call | bytes 3000000 | tf_op jit(solution)/shard_map/unpack/pallas_call | solution.py:351
  (3 shorter events, 0.0 us)
Async XLA Ops:
  0.0 16.3 %copy-start.2 = (s32[128,128]{1,0:T(8,128)S(1)}, s32[128,128]{1,0:T(8,128)}, u32[]{:S(2)}) copy-start(s32[128,128]{1,0:T(8,128)} %target.1) | copy-start | bytes 196612
  0.0 16.4 %copy-start.3 = (f32[5,5]{1,0:T(8,128)S(1)}, f32[5,5]{1,0:T(8,128)}, u32[]{:S(2)}) copy-start(f32[5,5]{1,0:T(8,128)} %coupling.1) | copy-start | bytes 304
  0.0 16.4 %copy-start.1 = (s32[1,48,64,128]{3,2,1,0:T(8,128)S(1)}, s32[1,48,64,128]{3,2,1,0:T(8,128)}, u32[]{:S(2)}) copy-start(s32[1,48,64,128]{3,2,1,0:T(8,128)} %param.11) | copy-start | bytes 4718596
  0.0 16.4 %copy-start = (f32[1,48,64,128]{3,2,1,0:T(8,128)S(1)}, f32[1,48,64,128]{3,2,1,0:T(8,128)}, u32[]{:S(2)}) copy-start(f32[1,48,64,128]{3,2,1,0:T(8,128)} %param.10) | copy-start | bytes 4718596
  11.1 17.7 %collective-permute-start = (f32[5,64,128]{2,1,0:T(8,128)}, f32[5,64,128]{2,1,0:T(8,128)S(1)}, u32[]{:S(2)}, u32[]{:S(2)}) collective-permute-start(f32[5,64,128]{2,1,0:T(8,128)} %get-tuple-element.14), channel_id=1, source_target_pairs={{0,1},{1,2},{2,3},{3,4},{4,5},{5,6},{6,7},{8,9},{9,10},{10,11},{11... | collective-permute-start | bytes 491528 | tf_op jit(solution)/shard_map/ppermute | solution.py:382
  15.0 13.8 %collective-permute-start.1 = (f32[5,64,128]{2,1,0:T(8,128)}, f32[5,64,128]{2,1,0:T(8,128)S(1)}, u32[]{:S(2)}, u32[]{:S(2)}) collective-permute-start(f32[5,64,128]{2,1,0:T(8,128)} %get-tuple-element.15), channel_id=1, source_target_pairs={{1,0},{2,1},{3,2},{4,3},{5,4},{6,5},{7,6},{9,8},{10,9},{11,10},{12... | collective-permute-start | bytes 491528 | tf_op jit(solution)/shard_map/ppermute | solution.py:383
  30.2 42.5 %all-to-all-start = ((f32[128,32,128]{2,1,0:T(8,128)}), f32[128,32,128]{2,1,0:T(8,128)S(1)}, u32[]{:S(2)}, u32[]{:S(2)}) async-start(f32[128,32,128]{2,1,0:T(8,128)} %bitcast.16), calls=%async_computation | async-start | bytes 4194304 | tf_op jit(solution)/shard_map/all_to_all | solution.py:390

commit v4 on v3

--- a/solution.py
+++ b/solution.py
@@ -8,7 +8,7 @@
 
 MIB = 1024 * 1024
 PLANES = 4
-AHEAD = 6
+AHEAD = 12
 PAD = 8
 
 
@@ -72,35 +72,35 @@
     return -(-rows // span)
 
 
-def face_kernel(state, first, last, sems):
-    cells_x = state.shape[1]
-    one = pltpu.make_async_copy(state.at[:, 0], first, sems.at[0])
-    two = pltpu.make_async_copy(state.at[:, cells_x - 1], last, sems.at[1])
+def face_kernel(odd, state, inner, outer, sems):
+    end = state.shape[1] - 1
+    one = pltpu.make_async_copy(state.at[:, end - end * odd[0]], inner, sems.at[0])
+    two = pltpu.make_async_copy(state.at[:, end * odd[0]], outer, sems.at[1])
     one.start()
     two.start()
     one.wait()
     two.wait()
 
 
-def faces_of(state):
+def faces_of(state, odd):
     fields, _, cells_y, lanes = state.shape
-    face = pltpu.HBM((fields, cells_y, lanes), jnp.float32)
-    hbm = pl.BlockSpec(memory_space=pltpu.HBM)
+    face = jax.ShapeDtypeStruct((fields, cells_y, lanes), jnp.float32)
+    vmem = pl.BlockSpec(memory_space=pltpu.VMEM)
     return pl.pallas_call(
         face_kernel,
         out_shape=(face, face),
-        in_specs=[hbm],
-        out_specs=(hbm, hbm),
+        in_specs=[pl.BlockSpec(memory_space=pltpu.SMEM), pl.BlockSpec(memory_space=pltpu.HBM)],
+        out_specs=(vmem, vmem),
         scratch_shapes=[pltpu.SemaphoreType.DMA((2,))],
         compiler_params=pltpu.CompilerParams(vmem_limit_bytes=2 * MIB),
         cost_estimate=pl.CostEstimate(flops=0, bytes_accessed=650_000, transcendentals=0),
         name="faces",
-    )(in_hbm(state))
+    )(odd.reshape(1), in_hbm(state))
 
 
 def main_kernel(
-    capacity, span, tile_rows, myself, coupling, target, state, adjoint, source, kv, fv,
-    sent, slots, ends, duals, out, stage, sv, av, bv, wv, pv, tv, seen, sems, tsem,
+    capacity, myself, coupling, target, state, adjoint, source, kv, fv,
+    out, slots, duals, sv, av, bv, wv, pv, tv, seen, sems, tsem,
 ):
     fields, cells_x, cells_y, lanes = adjoint.shape
     steps = cells_x // PLANES
@@ -165,22 +165,7 @@
             out[f, pl.ds(pl.multiple_of(at + PAD, 8), rows), :] = pooled[f * rows : (f + 1) * rows]
 
     copy(0, 0).wait()
-    edge = edge_tiles(rows, span)
-    batch = PLANES // 2 * rows // span
-
-    def place(first, count):
-        for i in range(count):
-            t = first + i
-            values = tile_values(
-                lambda f, d: out[f, pl.ds(PAD + span * t + d, 8), :], fields, span, tile_rows, lanes
-            )
-            send_tile(slots[t], t, values, stage, sent, tile_rows, tsem.at[1])
-
     def step_body(step, carry):
-        @pl.when(step >= 2)
-        def _():
-            place(edge + batch * (step - 2), batch)
-
         @pl.when(step + AHEAD < steps)
         def _():
             start(step + AHEAD)
@@ -220,41 +205,29 @@
 
     lax.fori_loop(0, steps, step_body, 0)
     pool(1, (cells_x // 2 - 1) * rows)
-    done = edge + batch * (steps - 2)
-    place(done, per_dev - edge - done)
     for i, x in enumerate((0, cells_x - 1)):
         for y in range(0, cells_y, 8):
             wgt = weight_of(fv[x, pl.ds(y, 8), :])
             for f in range(fields):
                 duals[i, f, pl.ds(y, 8), :] = wgt * av[f, x, pl.ds(y, 8), :]
-    kept = ends.shape[2]
-    for f in range(fields):
-        ends[0, f] = out[f, pl.ds(PAD, kept), :]
-        ends[1, f] = out[f, pl.ds(PAD + per_dev * span - kept, kept), :]
-    await_tiles(edge, per_dev - 2 * edge, stage, sent, tile_rows, tsem.at[1])
-
-
-def main_part(state, adjoint, source, kappa, flags, coupling, target, myself, capacity, span, tile_rows):
+
+def main_part(state, adjoint, source, kappa, flags, coupling, target, myself, capacity):
     fields, cells_x, cells_y, lanes = state.shape
     owners, per_dev = target.shape
-    kept = -(-edge_tiles(cells_y // 4, span) * span // 8) * 8
     f32 = jnp.float32
     hbm = pl.BlockSpec(memory_space=pltpu.HBM)
     vmem = pl.BlockSpec(memory_space=pltpu.VMEM)
     smem = pl.BlockSpec(memory_space=pltpu.SMEM)
     return pl.pallas_call(
-        functools.partial(main_kernel, capacity, span, tile_rows),
+        functools.partial(main_kernel, capacity),
         out_shape=(
-            pltpu.HBM((owners * capacity * tile_rows, lanes), f32),
+            jax.ShapeDtypeStruct((fields, cells_x * cells_y // 8 + 2 * PAD, lanes), f32),
             jax.ShapeDtypeStruct((per_dev,), jnp.int32),
-            pltpu.VMEM((2, fields, kept, lanes), f32),
-            pltpu.VMEM((2, fields, cells_y, lanes), f32),
+            jax.ShapeDtypeStruct((2, fields, cells_y, lanes), f32),
         ),
         in_specs=[smem, smem, hbm, hbm, hbm, hbm, vmem, vmem],
-        out_specs=(hbm, smem, vmem, vmem),
+        out_specs=(vmem, smem, vmem),
         scratch_shapes=[
-            pltpu.VMEM((fields, per_dev * span + 2 * PAD, lanes), f32),
-            pltpu.VMEM((per_dev * tile_rows, lanes), f32),
             pltpu.VMEM((fields, cells_x + 2, cells_y + 16, lanes), f32),
             pltpu.VMEM((fields, cells_x, cells_y, lanes), f32),
             pltpu.VMEM((fields, cells_x, cells_y, lanes), f32),
@@ -263,7 +236,7 @@
             pltpu.SMEM((8, per_dev), jnp.int32),
             pltpu.SMEM((owners,), jnp.int32),
             pltpu.SemaphoreType.DMA((cells_x // PLANES, 3)),
-            pltpu.SemaphoreType.DMA((2,)),
+            pltpu.SemaphoreType.DMA((1,)),
         ],
         compiler_params=pltpu.CompilerParams(vmem_limit_bytes=36 * MIB),
         cost_estimate=pl.CostEstimate(flops=100_000_000, bytes_accessed=27_700_000, transcendentals=0),
@@ -271,54 +244,65 @@
     )(myself, coupling, target, in_hbm(state), in_hbm(adjoint), in_hbm(source), kappa, flags)
 
 
-def edge_kernel(span, tile_rows, slots, ends, duals, before, after, sent, out, stage, pe, wv, pv, sem):
-    fields, cells_y, lanes = before.shape
+def pack_kernel(tile_rows, odd, slots, part, duals, inner, outer, out, stage, pe, wv, pv, sem):
+    fields, cells_y, lanes = inner.shape
     rows = cells_y // 4
     per_dev = slots.shape[0]
-    kept = ends.shape[2]
+    cells = part.shape[1] - 2 * PAD
+    span = cells // per_dev
+    kept = pe.shape[2] - 2 * PAD
     edge = edge_tiles(rows, span)
     pv[...] = pool_matrix(lanes)
-    for i, (face, at) in enumerate(((before, 0), (after, kept - rows))):
+    swapped = odd[0] != 0
+    for f in range(fields):
         for y in range(0, cells_y, 8):
-            for f in range(fields):
-                wv[i, f, pl.ds(y, 8), :] = duals[i, f, pl.ds(y, 8), :] * face[f, pl.ds(y, 8), :]
-        pooled = pooled_rows(wv.at[i], pv[...])
+            here = pl.ds(y, 8)
+            near, far = inner[f, here, :], outer[f, here, :]
+            wv[0, f, here, :] = duals[0, f, here, :] * jnp.where(swapped, near, far)
+            wv[1, f, here, :] = duals[1, f, here, :] * jnp.where(swapped, far, near)
+    pooled = [pooled_rows(wv.at[i], pv[...]) for i in range(2)]
+    for t in range(edge, per_dev - edge):
+        values = tile_values(
+            lambda f, d: part[f, pl.ds(PAD + span * t + d, 8), :], fields, span, tile_rows, lanes
+        )
+        send_tile(slots[t], t, values, stage, out, tile_rows, sem.at[0])
+    for i, (at, start) in enumerate(((0, 0), (kept - rows, cells - kept))):
         for f in range(fields):
-            pe[i, f, pl.ds(PAD, kept), :] = ends[i, f]
+            pe[i, f, pl.ds(PAD, kept), :] = part[f, pl.ds(PAD + start, kept), :]
             here = pl.ds(at + PAD, rows)
-            pe[i, f, here, :] = pe[i, f, here, :] + pooled[f * rows : (f + 1) * rows]
+            pe[i, f, here, :] = pe[i, f, here, :] + pooled[i][f * rows : (f + 1) * rows]
     for i, (tile, start) in enumerate(((0, 0), (per_dev - edge, kept - edge * span))):
         for k in range(edge):
             values = tile_values(
                 lambda f, d: pe[i, f, pl.ds(PAD + start + span * k + d, 8), :], fields, span, tile_rows, lanes
             )
-            send_tile(slots[tile + k], i * edge + k, values, stage, out, tile_rows, sem.at[0])
-    await_tiles(0, 2 * edge, stage, out, tile_rows, sem.at[0])
-
-
-def edge_part(sent, slots, ends, duals, before, after, span, tile_rows):
-    fields, cells_y, lanes = before.shape
+            send_tile(slots[tile + k], tile + k, values, stage, out, tile_rows, sem.at[0])
+    await_tiles(0, per_dev, stage, out, tile_rows, sem.at[0])
+
+
+def pack_part(odd, part, slots, duals, inner, outer, n_slots, tile_rows):
+    fields, cells_y, lanes = inner.shape
+    per_dev = slots.shape[0]
+    span = (part.shape[1] - 2 * PAD) // per_dev
+    kept = -(-edge_tiles(cells_y // 4, span) * span // 8) * 8
     f32 = jnp.float32
     vmem = pl.BlockSpec(memory_space=pltpu.VMEM)
-    hbm = pl.BlockSpec(memory_space=pltpu.HBM)
-    edge = edge_tiles(cells_y // 4, span)
     return pl.pallas_call(
-        functools.partial(edge_kernel, span, tile_rows),
-        out_shape=pltpu.HBM(sent.shape, f32),
-        in_specs=[pl.BlockSpec(memory_space=pltpu.SMEM), vmem, vmem, vmem, vmem, hbm],
-        out_specs=hbm,
+        functools.partial(pack_kernel, tile_rows),
+        out_shape=pltpu.HBM((n_slots * tile_rows, lanes), f32),
+        in_specs=[pl.BlockSpec(memory_space=pltpu.SMEM)] * 2 + [vmem] * 4,
+        out_specs=pl.BlockSpec(memory_space=pltpu.HBM),
         scratch_shapes=[
-            pltpu.VMEM((2 * edge * tile_rows, lanes), f32),
-            pltpu.VMEM((2, fields, ends.shape[2] + 2 * PAD, lanes), f32),
+            pltpu.VMEM((per_dev * tile_rows, lanes), f32),
+            pltpu.VMEM((2, fields, kept + 2 * PAD, lanes), f32),
             pltpu.VMEM((2, fields, cells_y, lanes), f32),
             pltpu.VMEM((2 * lanes, lanes), jnp.bfloat16),
             pltpu.SemaphoreType.DMA((1,)),
         ],
-        input_output_aliases={5: 0},
         compiler_params=pltpu.CompilerParams(vmem_limit_bytes=12 * MIB),
-        cost_estimate=pl.CostEstimate(flops=1_000_000, bytes_accessed=100_000, transcendentals=0),
-        name="edges",
-    )(slots, ends, duals, before, after, in_hbm(sent))
+        cost_estimate=pl.CostEstimate(flops=1_000_000, bytes_accessed=3_500_000, transcendentals=0),
+        name="edges_pack",
+    )(odd, slots, part, duals, inner, outer)
 
 
 def unpack_kernel(tile_rows, lookup, received, out, stage, built, sems):
@@ -376,16 +360,17 @@
     tile_rows = -(-span * fields // 8) * 8
     myself = lax.axis_index(("grp", "brk"))
 
-    up = [(i, i + 1) for i in range(bricks - 1)]
-    down = [(j, i) for i, j in up]
-    first, last = faces_of(state)
-    before = lax.ppermute(last, "brk", up)
-    after = lax.ppermute(first, "brk", down)
-
-    sent, slots, ends, duals = main_part(
-        state, adjoint, source, kappa, flags, coupling, target, myself.reshape(1), capacity, span, tile_rows
+    odd = lax.rem(lax.axis_index("brk"), 2)
+    one = [(i, i ^ 1) for i in range(bricks)]
+    two = [(i, j) for i in range(1, bricks - 1) for j in (((i - 1) ^ 1) + 1,)]
+    faces = faces_of(state, odd)
+    inner = lax.ppermute(faces[0], "brk", one)
+    outer = lax.ppermute(faces[1], "brk", two)
+
+    part, slots, duals = main_part(
+        state, adjoint, source, kappa, flags, coupling, target, myself.reshape(1), capacity
     )
-    outgoing = edge_part(sent, slots, ends, duals, before, after, span, tile_rows)
+    outgoing = pack_part(odd.reshape(1), part, slots, duals, inner, outer, owners * capacity, tile_rows)
     outgoing = outgoing.reshape(owners, capacity * tile_rows, lanes)
     incoming = lax.all_to_all(outgoing, ("grp", "brk"), 0, 0, tiled=True)
     incoming = incoming.reshape(owners * capacity * tile_rows, lanes)

time: 74.6 us -> 62.3 us (0.84)
  Pallas kernels: 26.5 us -> 15.7 us
  starting transfers between devices: 17.4 us -> 15.8 us
    pallas_call x3, Pallas kernels: 24.9 us -> 14 us  [the longest x1 10.4 us: main_part(): pl.pallas_call(functools.partial(main_kernel, capacity), out_shape=(jax.S...]
    ppermute x2, starting transfers between devices: 5.25 us -> 2.78 us  [the longest x1 2.12 us: local(): inner = lax.ppermute(faces[0], 'brk', one)]
    all_to_all x1, starting transfers between devices: 12.1 us -> 13.1 us  [local(): incoming = lax.all_to_all(outgoing, ('grp', 'brk'), 0, 0, tiled=True)]
where the time goes in v4:
time: 62.3 us; the launch traced here: 62.1 us
  waiting for transfers between devices  28.9 us (46%)
  starting transfers between devices  15.8 us (25%)
  Pallas kernels  15.7 us (25%)
  other arithmetic  1.53 us (2%)
    all_to_all x1, waiting for transfers between devices, local(): incoming = lax.all_to_all(outgoing, ('grp', 'brk'), 0, 0, tiled=True)  28.9 us
    all_to_all x1, starting transfers between devices, local(): incoming = lax.all_to_all(outgoing, ('grp', 'brk'), 0, 0, tiled=True)  13.1 us
    pallas_call x1, Pallas kernels, main_part(): pl.pallas_call(functools.partial(main_kernel, capacity), out_shape=(jax.S...  10.4 us
    ppermute x1, starting transfers between devices, local(): inner = lax.ppermute(faces[0], 'brk', one)  2.12 us
    pallas_call x1, Pallas kernels, faces_of(): pl.pallas_call(face_kernel, out_shape=(face, face), in_specs=[pl.BlockSpe...  1.87 us
    pallas_call x1, Pallas kernels, pack_part(): pl.pallas_call(functools.partial(pack_kernel, tile_rows), out_shape=pltpu...  1.76 us
    pallas_call x1, Pallas kernels, unpack_part(): pl.pallas_call(functools.partial(unpack_kernel, tile_rows), out_shape=jax...  1.72 us
    reduce_sum x1, other arithmetic, local(): origin = jnp.sum(jnp.where(hit, codes[None, :], 0), axis=1)  1.32 us
  transfers between devices with their start and end apart: 3, of which 1 were waited for; matrix products, arithmetic and copies ran while one was open for 2% of the time, Pallas kernels for 17%

profile of v4, /device:TPU:1, one launch (start us, length us, event | category | flops | bytes accessed | tf_op | source)
XLA Modules:
  0.0 62.1 jit_solution(896998452572964796)
XLA Ops:
  0.0 0.0 copy-start.2
  0.0 0.0 copy-start.3
  0.0 0.0 copy-start.1
  0.0 0.0 copy-start
  0.0 1.9 %faces.1 = (f32[5,64,128]{2,1,0:T(8,128)}, f32[5,64,128]{2,1,0:T(8,128)}) custom-call(s32[1]{0:T(128)} %bitcast.1.odd, f32[5,48,64,128]{3,2,1,0:T(8,128)} %bitcast.15), custom_call_target="tpu_custom_call" | custom-call | bytes 650000 | tf_op jit(solution)/shard_map/faces/pallas_call | solution.py:89
  1.9 2.1 %collective-permute-start = (f32[5,64,128]{2,1,0:T(8,128)}, f32[5,64,128]{2,1,0:T(8,128)S(1)}, u32[]{:S(2)}, u32[]{:S(2)}) collective-permute-start(f32[5,64,128]{2,1,0:T(8,128)} %get-tuple-element.13), channel_id=1, source_target_pairs={{0,1},{1,0},{2,3},{3,2},{4,5},{5,4},{6,7},{7,6},{8,9},{9,8},{10,11... | collective-permute-start | bytes 491528 | tf_op jit(solution)/shard_map/ppermute | solution.py:367
  4.0 0.7 %collective-permute-start.1 = (f32[5,64,128]{2,1,0:T(8,128)}, f32[5,64,128]{2,1,0:T(8,128)S(1)}, u32[]{:S(2)}, u32[]{:S(2)}) collective-permute-start(f32[5,64,128]{2,1,0:T(8,128)} %get-tuple-element.14), channel_id=1, source_target_pairs={{1,2},{2,1},{3,4},{4,3},{5,6},{6,5},{9,10},{10,9},{11,12},{12,11},... | collective-permute-start | bytes 491528 | tf_op jit(solution)/shard_map/ppermute | solution.py:368
  4.7 0.0 copy-done.2
  4.7 0.0 copy-done.3
  4.7 0.0 copy-done.1
  4.7 0.0 copy-done
  4.7 10.4 %residual_pool.1 = (f32[5,400,128]{2,1,0:T(8,128)S(1)}, s32[128]{0:T(128)S(1)}, f32[2,5,64,128]{3,2,1,0:T(8,128)S(1)}) custom-call(s32[1]{0:T(128)} %bitcast.2.myself, f32[5,5]{1,0:T(8,128)S(1)} %copy-done.3, s32[128,128]{1,0:T(8,128)S(1)} %copy-done.2, f32[5,48,64,128]{3,2,1,0:T(8,128)} %bitcast.16, f32[5,48,64,128]{3,2,1,0:T(8,128)} %bitcast.18, ...), custom_call_target="tpu_custom_call" | custom-call | flops 100000000 | bytes 27700000 | tf_op jit(solution)/shard_map/residual_pool/pallas_call | solution.py:221
  15.1 0.0 collective-permute-done.inner
  15.2 0.0 collective-permute-done.1.outer
  15.2 1.8 %edges_pack.1 = f32[4096,128]{1,0:T(8,128)} custom-call(s32[1]{0:T(128)} %bitcast.1.odd, s32[128]{0:T(128)S(1)} %get-tuple-element.10.slots, f32[5,400,128]{2,1,0:T(8,128)S(1)} %get-tuple-element.11.part, f32[2,5,64,128]{3,2,1,0:T(8,128)S(1)} %get-tuple-element.12.duals, f32[5,64,128]{2,1,0:T(8,128)S(1)} %collective-permute-done.inner, ...), custom_call_target="tpu_custom_call" | custom-call | flops 1000000 | bytes 3500000 | tf_op jit(solution)/shard_map/edges_pack/pallas_call | solution.py:290
  16.9 13.1 %all-to-all-start = ((f32[128,32,128]{2,1,0:T(8,128)}), f32[128,32,128]{2,1,0:T(8,128)S(1)}, u32[]{:S(2)}, u32[]{:S(2)}) async-start(f32[128,32,128]{2,1,0:T(8,128)} %bitcast.17), calls=%async_computation | async-start | bytes 4194304 | tf_op jit(solution)/shard_map/all_to_all | solution.py:375
  30.0 1.3 %select_reduce_fusion = s32[128]{0:T(128)S(1)} fusion(s32[16384]{0:T(1024)S(1)} %bitcast.14, s32[128]{0:T(128)S(1)} %iota_add_fusion), kind=kLoop, calls=%fused_computation | loop fusion | flops 6291328 | bytes 66560 | tf_op jit(solution)/shard_map/reduce_sum | solution.py:381
  31.3 0.2 convert_reduce_fusion
  31.6 28.9 %all-to-all-done = f32[128,32,128]{2,1,0:T(8,128)S(1)} async-done(((f32[128,32,128]{2,1,0:T(8,128)}), f32[128,32,128]{2,1,0:T(8,128)S(1)}, u32[]{:S(2)}, u32[]{:S(2)}) %all-to-all-start) | async-done | bytes 2097184 | tf_op jit(solution)/shard_map/all_to_all | solution.py:375
  60.4 1.7 %unpack.1 = f32[5,128,384]{2,1,0:T(8,128)} custom-call(s32[128]{0:T(128)S(1)} %multiply_add_fusion.lookup, f32[4096,128]{1,0:T(8,128)S(1)} %bitcast.11), custom_call_target="tpu_custom_call" | custom-call | bytes 3000000 | tf_op jit(solution)/shard_map/unpack/pallas_call | solution.py:335
  (3 shorter events, 0.0 us)
Async XLA Ops:
  0.0 4.7 %copy-start.2 = (s32[128,128]{1,0:T(8,128)S(1)}, s32[128,128]{1,0:T(8,128)}, u32[]{:S(2)}) copy-start(s32[128,128]{1,0:T(8,128)} %target.1) | copy-start | bytes 196612
  0.0 4.7 %copy-start.3 = (f32[5,5]{1,0:T(8,128)S(1)}, f32[5,5]{1,0:T(8,128)}, u32[]{:S(2)}) copy-start(f32[5,5]{1,0:T(8,128)} %coupling.1) | copy-start | bytes 304
  0.0 4.7 %copy-start.1 = (s32[1,48,64,128]{3,2,1,0:T(8,128)S(1)}, s32[1,48,64,128]{3,2,1,0:T(8,128)}, u32[]{:S(2)}) copy-start(s32[1,48,64,128]{3,2,1,0:T(8,128)} %param.11) | copy-start | bytes 4718596
  0.0 4.7 %copy-start = (f32[1,48,64,128]{3,2,1,0:T(8,128)S(1)}, f32[1,48,64,128]{3,2,1,0:T(8,128)}, u32[]{:S(2)}) copy-start(f32[1,48,64,128]{3,2,1,0:T(8,128)} %param.10) | copy-start | bytes 4718596
  1.9 13.2 %collective-permute-start = (f32[5,64,128]{2,1,0:T(8,128)}, f32[5,64,128]{2,1,0:T(8,128)S(1)}, u32[]{:S(2)}, u32[]{:S(2)}) collective-permute-start(f32[5,64,128]{2,1,0:T(8,128)} %get-tuple-element.13), channel_id=1, source_target_pairs={{0,1},{1,0},{2,3},{3,2},{4,5},{5,4},{6,7},{7,6},{8,9},{9,8},{10,11... | collective-permute-start | bytes 491528 | tf_op jit(solution)/shard_map/ppermute | solution.py:367
  4.0 11.1 %collective-permute-start.1 = (f32[5,64,128]{2,1,0:T(8,128)}, f32[5,64,128]{2,1,0:T(8,128)S(1)}, u32[]{:S(2)}, u32[]{:S(2)}) collective-permute-start(f32[5,64,128]{2,1,0:T(8,128)} %get-tuple-element.14), channel_id=1, source_target_pairs={{1,2},{2,1},{3,4},{4,3},{5,6},{6,5},{9,10},{10,9},{11,12},{12,11},... | collective-permute-start | bytes 491528 | tf_op jit(solution)/shard_map/ppermute | solution.py:368
  16.9 43.5 %all-to-all-start = ((f32[128,32,128]{2,1,0:T(8,128)}), f32[128,32,128]{2,1,0:T(8,128)S(1)}, u32[]{:S(2)}, u32[]{:S(2)}) async-start(f32[128,32,128]{2,1,0:T(8,128)} %bitcast.17), calls=%async_computation | async-start | bytes 4194304 | tf_op jit(solution)/shard_map/all_to_all | solution.py:375

commit v5 on v4

--- a/solution.py
+++ b/solution.py
@@ -72,35 +72,35 @@
     return -(-rows // span)
 
 
-def face_kernel(odd, state, inner, outer, sems):
-    end = state.shape[1] - 1
-    one = pltpu.make_async_copy(state.at[:, end - end * odd[0]], inner, sems.at[0])
-    two = pltpu.make_async_copy(state.at[:, end * odd[0]], outer, sems.at[1])
+def face_kernel(state, first, last, sems):
+    cells_x = state.shape[1]
+    one = pltpu.make_async_copy(state.at[:, 0], first, sems.at[0])
+    two = pltpu.make_async_copy(state.at[:, cells_x - 1], last, sems.at[1])
     one.start()
     two.start()
     one.wait()
     two.wait()
 
 
-def faces_of(state, odd):
+def faces_of(state):
     fields, _, cells_y, lanes = state.shape
     face = jax.ShapeDtypeStruct((fields, cells_y, lanes), jnp.float32)
     vmem = pl.BlockSpec(memory_space=pltpu.VMEM)
     return pl.pallas_call(
         face_kernel,
         out_shape=(face, face),
-        in_specs=[pl.BlockSpec(memory_space=pltpu.SMEM), pl.BlockSpec(memory_space=pltpu.HBM)],
+        in_specs=[pl.BlockSpec(memory_space=pltpu.HBM)],
         out_specs=(vmem, vmem),
         scratch_shapes=[pltpu.SemaphoreType.DMA((2,))],
         compiler_params=pltpu.CompilerParams(vmem_limit_bytes=2 * MIB),
         cost_estimate=pl.CostEstimate(flops=0, bytes_accessed=650_000, transcendentals=0),
         name="faces",
-    )(odd.reshape(1), in_hbm(state))
+    )(in_hbm(state))
 
 
 def main_kernel(
-    capacity, myself, coupling, target, state, adjoint, source, kv, fv,
-    out, slots, duals, sv, av, bv, wv, pv, tv, seen, sems, tsem,
+    capacity, myself, coupling, target, state, adjoint, source, kappa, flags,
+    out, slots, duals, sv, av, bv, kv, fv, wv, pv, tv, seen, sems, tsem,
 ):
     fields, cells_x, cells_y, lanes = adjoint.shape
     steps = cells_x // PLANES
@@ -112,11 +112,14 @@
         if i == 0:
             landing = sv.at[:, pl.ds(PLANES * step + 1, PLANES), pl.ds(8, cells_y)]
             return pltpu.make_async_copy(state.at[:, at], landing, sems.at[step, 0])
+        if i > 2:
+            src, dst = ((kappa, kv), (flags, fv))[i - 3]
+            return pltpu.make_async_copy(src.at[at], dst.at[at], sems.at[step, i])
         src, dst = ((adjoint, av), (source, bv))[i - 1]
         return pltpu.make_async_copy(src.at[:, at], dst.at[:, at], sems.at[step, i])
 
     def start(step):
-        for i in range(3):
+        for i in range(5):
             copy(step, i).start()
 
     me = myself[0]
@@ -174,8 +177,8 @@
         def _():
             copy(step + 1, 0).wait()
 
-        copy(step, 1).wait()
-        copy(step, 2).wait()
+        for i in range(1, 5):
+            copy(step, i).wait()
 
         for half in range(PLANES // 2):
             coarse = step * (PLANES // 2) + half
@@ -225,23 +228,25 @@
             jax.ShapeDtypeStruct((per_dev,), jnp.int32),
             jax.ShapeDtypeStruct((2, fields, cells_y, lanes), f32),
         ),
-        in_specs=[smem, smem, hbm, hbm, hbm, hbm, vmem, vmem],
+        in_specs=[smem, smem, hbm, hbm, hbm, hbm, hbm, hbm],
         out_specs=(vmem, smem, vmem),
         scratch_shapes=[
             pltpu.VMEM((fields, cells_x + 2, cells_y + 16, lanes), f32),
             pltpu.VMEM((fields, cells_x, cells_y, lanes), f32),
             pltpu.VMEM((fields, cells_x, cells_y, lanes), f32),
+            pltpu.VMEM((cells_x, cells_y, lanes), f32),
+            pltpu.VMEM((cells_x, cells_y, lanes), jnp.int32),
             pltpu.VMEM((2, fields, cells_y, lanes), f32),
             pltpu.VMEM((2 * lanes, lanes), jnp.bfloat16),
             pltpu.SMEM((8, per_dev), jnp.int32),
             pltpu.SMEM((owners,), jnp.int32),
-            pltpu.SemaphoreType.DMA((cells_x // PLANES, 3)),
+            pltpu.SemaphoreType.DMA((cells_x // PLANES, 5)),
             pltpu.SemaphoreType.DMA((1,)),
         ],
         compiler_params=pltpu.CompilerParams(vmem_limit_bytes=36 * MIB),
         cost_estimate=pl.CostEstimate(flops=100_000_000, bytes_accessed=27_700_000, transcendentals=0),
         name="residual_pool",
-    )(myself, coupling, target, in_hbm(state), in_hbm(adjoint), in_hbm(source), kappa, flags)
+    )(myself, in_hbm(coupling), in_hbm(target), in_hbm(state), in_hbm(adjoint), in_hbm(source), in_hbm(kappa), in_hbm(flags))
 
 
 def pack_kernel(tile_rows, odd, slots, part, duals, inner, outer, out, stage, pe, wv, pv, sem):
@@ -319,10 +324,10 @@
         buf = stage.at[g % stage.shape[0]]
         for s in range(8):
             base = pl.multiple_of(lookup[g * 8 + s] * tile_rows, 8)
-            buf[pl.ds(s * tile_rows, tile_rows), :] = received[pl.ds(base, tile_rows), :]
+            buf[pl.ds(s * (tile_rows + 1), tile_rows), :] = received[pl.ds(base, tile_rows), :]
         for f in range(fields):
             for j in range(span):
-                rows = buf[pl.ds(f * span + j, 8, stride=tile_rows), :]
+                rows = buf[pl.ds(f * span + j, 8, stride=tile_rows + 1), :]
                 built[f, pl.ds(g * 8, 8), pl.ds(j * lanes, lanes)] = rows
         if (g + 1) * 8 % piece == 0:
             leave(g * 8 // piece).start()
@@ -338,7 +343,7 @@
         in_specs=[pl.BlockSpec(memory_space=pltpu.SMEM), pl.BlockSpec(memory_space=pltpu.VMEM)],
         out_specs=pl.BlockSpec(memory_space=pltpu.HBM),
         scratch_shapes=[
-            pltpu.VMEM((4, 8 * tile_rows, lanes), jnp.float32),
+            pltpu.VMEM((4, 8 * (tile_rows + 1), lanes), jnp.float32),
             pltpu.VMEM((fields, per_dev, width), jnp.float32),
             pltpu.SemaphoreType.DMA((4,)),
         ],
@@ -363,9 +368,11 @@
     odd = lax.rem(lax.axis_index("brk"), 2)
     one = [(i, i ^ 1) for i in range(bricks)]
     two = [(i, j) for i in range(1, bricks - 1) for j in (((i - 1) ^ 1) + 1,)]
-    faces = faces_of(state, odd)
-    inner = lax.ppermute(faces[0], "brk", one)
-    outer = lax.ppermute(faces[1], "brk", two)
+    planes = state.reshape(fields * cells_x, cells_y, lanes)
+    first = lax.slice(planes, (0, 0, 0), planes.shape, (cells_x, 1, 1))
+    last = lax.slice(planes, (cells_x - 1, 0, 0), planes.shape, (cells_x, 1, 1))
+    inner = lax.ppermute(jnp.where(odd == 0, last, first), "brk", one)
+    outer = lax.ppermute(jnp.where(odd == 0, first, last), "brk", two)
 
     part, slots, duals = main_part(
         state, adjoint, source, kappa, flags, coupling, target, myself.reshape(1), capacity

time: 62.3 us -> 61.9 us (level)
  Pallas kernels: 15.7 us -> 14.2 us
  other arithmetic: 1.53 us -> 2.55 us
    ppermute x2, starting transfers between devices: 2.78 us -> 5.24 us  [the longest x1 4.57 us: local(): inner = lax.ppermute(jnp.where(odd == 0, last, first), 'brk', one)]
    all_to_all x1, starting transfers between devices: 13.1 us -> 10.6 us  [local(): incoming = lax.all_to_all(outgoing, ('grp', 'brk'), 0, 0, tiled=True)]
    pallas_call x1 -> x0, Pallas kernels: 1.87 us -> none  [faces_of(): pl.pallas_call(face_kernel, out_shape=(face, face), in_specs=[pl.BlockSpe...]
    select_n x0 -> x1, other arithmetic: none -> 1.02 us  [local(): outer = lax.ppermute(jnp.where(odd == 0, first, last), 'brk', two)]
  transfers between devices with their start and end apart: 3 -> 3, of which waited for: 1 -> 1; matrix products, arithmetic and copies ran while one was open for 2% -> 2% of each run, Pallas kernels for 17% -> 18%
where the time goes in v5:
time: 61.9 us; the launch traced here: 61.6 us
  waiting for transfers between devices  28.8 us (47%)
  starting transfers between devices  15.9 us (26%)
  Pallas kernels  14.2 us (23%)
  other arithmetic  2.55 us (4%)
    all_to_all x1, waiting for transfers between devices, local(): incoming = lax.all_to_all(outgoing, ('grp', 'brk'), 0, 0, tiled=True)  28.8 us
    pallas_call x1, Pallas kernels, main_part(): pl.pallas_call(functools.partial(main_kernel, capacity), out_shape=(jax.S...  10.9 us
    all_to_all x1, starting transfers between devices, local(): incoming = lax.all_to_all(outgoing, ('grp', 'brk'), 0, 0, tiled=True)  10.6 us
    ppermute x1, starting transfers between devices, local(): inner = lax.ppermute(jnp.where(odd == 0, last, first), 'brk', one)  4.57 us
    pallas_call x1, Pallas kernels, pack_part(): pl.pallas_call(functools.partial(pack_kernel, tile_rows), out_shape=pltpu...  1.73 us
    pallas_call x1, Pallas kernels, unpack_part(): pl.pallas_call(functools.partial(unpack_kernel, tile_rows), out_shape=jax...  1.56 us
    reduce_sum x1, other arithmetic, local(): origin = jnp.sum(jnp.where(hit, codes[None, :], 0), axis=1)  1.32 us
  transfers between devices with their start and end apart: 3, of which 1 were waited for; matrix products, arithmetic and copies ran while one was open for 2% of the time, Pallas kernels for 18%

profile of v5, /device:TPU:1, one launch (start us, length us, event | category | flops | bytes accessed | tf_op | source)
XLA Modules:
  0.0 61.6 jit_solution(4899590665916645385)
XLA Ops:
  0.0 1.0 %slice_select_fusion = (f32[5,64,128]{2,1,0:T(8,128)S(1)}, f32[5,64,128]{2,1,0:T(8,128)S(1)}) fusion(f32[240,64,128]{2,1,0:T(8,128)} %bitcast.13, pred[]{:T(512)S(6)} %eq.39), kind=kLoop, calls=%fused_computation.1 | loop fusion | flops 81920 | bytes 655361 | tf_op jit(solution)/shard_map/jit(_where)/select_n | solution.py:375
  1.0 0.7 %collective-permute-start.1 = (f32[5,64,128]{2,1,0:T(8,128)S(1)}, f32[5,64,128]{2,1,0:T(8,128)S(1)}, u32[]{:S(2)}, u32[]{:S(2)}) collective-permute-start(f32[5,64,128]{2,1,0:T(8,128)S(1)} %get-tuple-element.11), channel_id=1, source_target_pairs={{1,2},{2,1},{3,4},{4,3},{5,6},{6,5},{9,10},{10,9},{11,12},{12,11},... | collective-permute-start | bytes 491528 | tf_op jit(solution)/shard_map/ppermute | solution.py:375
  1.7 4.6 %collective-permute-start = (f32[5,64,128]{2,1,0:T(8,128)S(1)}, f32[5,64,128]{2,1,0:T(8,128)S(1)}, u32[]{:S(2)}, u32[]{:S(2)}) collective-permute-start(f32[5,64,128]{2,1,0:T(8,128)S(1)} %get-tuple-element.12), channel_id=1, source_target_pairs={{0,1},{1,0},{2,3},{3,2},{4,5},{5,4},{6,7},{7,6},{8,9},{9,8},{10,11... | collective-permute-start | bytes 491528 | tf_op jit(solution)/shard_map/ppermute | solution.py:374
  6.3 10.9 %residual_pool.1 = (f32[5,400,128]{2,1,0:T(8,128)S(1)}, s32[128]{0:T(128)S(1)}, f32[2,5,64,128]{3,2,1,0:T(8,128)S(1)}) custom-call(s32[1]{0:T(128)} %bitcast.2.myself, f32[5,5]{1,0:T(8,128)} %coupling.1, s32[128,128]{1,0:T(8,128)} %target.1, f32[5,48,64,128]{3,2,1,0:T(8,128)} %bitcast.14, f32[5,48,64,128]{3,2,1,0:T(8,128)} %bitcast.16, ...), custom_call_target="tpu_custom_call" | custom-call | flops 100000000 | bytes 27700000 | tf_op jit(solution)/shard_map/residual_pool/pallas_call | solution.py:224
  17.2 0.0 copy-start
  17.2 0.0 collective-permute-done.1.outer
  17.2 0.0 collective-permute-done.inner
  17.2 1.7 %edges_pack.1 = f32[4096,128]{1,0:T(8,128)} custom-call(s32[1]{0:T(128)} %bitcast.1.odd, s32[128]{0:T(128)S(1)} %get-tuple-element.8.slots, f32[5,400,128]{2,1,0:T(8,128)S(1)} %get-tuple-element.9.part, f32[2,5,64,128]{3,2,1,0:T(8,128)S(1)} %get-tuple-element.10.duals, f32[5,64,128]{2,1,0:T(8,128)S(1)} %collective-permute-done.inner, ...), custom_call_target="tpu_custom_call" | custom-call | flops 1000000 | bytes 3500000 | tf_op jit(solution)/shard_map/edges_pack/pallas_call | solution.py:295
  19.0 10.6 %all-to-all-start = ((f32[128,32,128]{2,1,0:T(8,128)}), f32[128,32,128]{2,1,0:T(8,128)S(1)}, u32[]{:S(2)}, u32[]{:S(2)}) async-start(f32[128,32,128]{2,1,0:T(8,128)} %bitcast.15), calls=%async_computation | async-start | bytes 4194304 | tf_op jit(solution)/shard_map/all_to_all | solution.py:382
  29.6 0.0 copy-done
  29.6 1.3 %select_reduce_fusion = s32[128]{0:T(128)S(1)} fusion(s32[16384]{0:T(1024)S(1)} %bitcast.20, s32[128]{0:T(128)S(1)} %iota_add_fusion), kind=kLoop, calls=%fused_computation | loop fusion | flops 6291328 | bytes 66560 | tf_op jit(solution)/shard_map/reduce_sum | solution.py:388
  31.0 0.2 convert_reduce_fusion
  31.2 28.8 %all-to-all-done = f32[128,32,128]{2,1,0:T(8,128)S(1)} async-done(((f32[128,32,128]{2,1,0:T(8,128)}), f32[128,32,128]{2,1,0:T(8,128)S(1)}, u32[]{:S(2)}, u32[]{:S(2)}) %all-to-all-start) | async-done | bytes 2097184 | tf_op jit(solution)/shard_map/all_to_all | solution.py:382
  60.0 1.6 %unpack.1 = f32[5,128,384]{2,1,0:T(8,128)} custom-call(s32[128]{0:T(128)S(1)} %multiply_add_fusion.lookup, f32[4096,128]{1,0:T(8,128)S(1)} %bitcast.12), custom_call_target="tpu_custom_call" | custom-call | bytes 3000000 | tf_op jit(solution)/shard_map/unpack/pallas_call | solution.py:340
  (3 shorter events, 0.0 us)
Async XLA Ops:
  1.0 16.2 %collective-permute-start.1 = (f32[5,64,128]{2,1,0:T(8,128)S(1)}, f32[5,64,128]{2,1,0:T(8,128)S(1)}, u32[]{:S(2)}, u32[]{:S(2)}) collective-permute-start(f32[5,64,128]{2,1,0:T(8,128)S(1)} %get-tuple-element.11), channel_id=1, source_target_pairs={{1,2},{2,1},{3,4},{4,3},{5,6},{6,5},{9,10},{10,9},{11,12},{12,11},... | collective-permute-start | bytes 491528 | tf_op jit(solution)/shard_map/ppermute | solution.py:375
  1.7 15.5 %collective-permute-start = (f32[5,64,128]{2,1,0:T(8,128)S(1)}, f32[5,64,128]{2,1,0:T(8,128)S(1)}, u32[]{:S(2)}, u32[]{:S(2)}) collective-permute-start(f32[5,64,128]{2,1,0:T(8,128)S(1)} %get-tuple-element.12), channel_id=1, source_target_pairs={{0,1},{1,0},{2,3},{3,2},{4,5},{5,4},{6,7},{7,6},{8,9},{9,8},{10,11... | collective-permute-start | bytes 491528 | tf_op jit(solution)/shard_map/ppermute | solution.py:374
  17.2 12.4 %copy-start = (s32[128,128]{1,0:T(8,128)S(1)}, s32[128,128]{1,0:T(8,128)}, u32[]{:S(2)}) copy-start(s32[128,128]{1,0:T(8,128)} %target.1) | copy-start | bytes 196612
  19.0 41.0 %all-to-all-start = ((f32[128,32,128]{2,1,0:T(8,128)}), f32[128,32,128]{2,1,0:T(8,128)S(1)}, u32[]{:S(2)}, u32[]{:S(2)}) async-start(f32[128,32,128]{2,1,0:T(8,128)} %bitcast.15), calls=%async_computation | async-start | bytes 4194304 | tf_op jit(solution)/shard_map/all_to_all | solution.py:382

commit v6 on v5

--- a/solution.py
+++ b/solution.py
@@ -8,7 +8,6 @@
 
 MIB = 1024 * 1024
 PLANES = 4
-AHEAD = 12
 PAD = 8
 
 
@@ -119,15 +118,19 @@
         return pltpu.make_async_copy(src.at[:, at], dst.at[:, at], sems.at[step, i])
 
     def start(step):
-        for i in range(5):
+        copy(step + 1, 0).start()
+        for i in range(1, 5):
             copy(step, i).start()
 
     me = myself[0]
     row8 = pl.multiple_of(lax.shift_left(lax.shift_right_logical(me, 3), 3), 8)
     table = pltpu.make_async_copy(target.at[pl.ds(row8, 8)], tv, tsem.at[0])
     table.start()
-    for step in range(AHEAD):
+    copy(0, 0).start()
+    for step in range(steps - 1):
         start(step)
+    for i in range(1, 5):
+        copy(steps - 1, i).start()
     zero = jnp.zeros((8, lanes), jnp.float32)
     pv[...] = pool_matrix(lanes)
 
@@ -169,10 +172,6 @@
 
     copy(0, 0).wait()
     def step_body(step, carry):
-        @pl.when(step + AHEAD < steps)
-        def _():
-            start(step + AHEAD)
-
         @pl.when(step + 1 < steps)
         def _():
             copy(step + 1, 0).wait()

time: 61.9 us -> 61.6 us (level)
  transfers between devices with their start and end apart: 3 -> 3, of which waited for: 1 -> 1; matrix products, arithmetic and copies ran while one was open for 2% -> 2% of each run, Pallas kernels for 18% -> 17%
where the time goes in v6:
time: 61.6 us; the launch traced here: 61.3 us
  waiting for transfers between devices  28.8 us (47%)
  starting transfers between devices  15.9 us (26%)
  Pallas kernels  13.9 us (23%)
  other arithmetic  2.55 us (4%)
    all_to_all x1, waiting for transfers between devices, local(): incoming = lax.all_to_all(outgoing, ('grp', 'brk'), 0, 0, tiled=True)  28.8 us
    all_to_all x1, starting transfers between devices, local(): incoming = lax.all_to_all(outgoing, ('grp', 'brk'), 0, 0, tiled=True)  10.7 us
    pallas_call x1, Pallas kernels, main_part(): pl.pallas_call(functools.partial(main_kernel, capacity), out_shape=(jax.S...  10.6 us
    ppermute x1, starting transfers between devices, local(): inner = lax.ppermute(jnp.where(odd == 0, last, first), 'brk', one)  4.57 us
    pallas_call x1, Pallas kernels, pack_part(): pl.pallas_call(functools.partial(pack_kernel, tile_rows), out_shape=pltpu...  1.72 us
    pallas_call x1, Pallas kernels, unpack_part(): pl.pallas_call(functools.partial(unpack_kernel, tile_rows), out_shape=jax...  1.56 us
    reduce_sum x1, other arithmetic, local(): origin = jnp.sum(jnp.where(hit, codes[None, :], 0), axis=1)  1.32 us
  transfers between devices with their start and end apart: 3, of which 1 were waited for; matrix products, arithmetic and copies ran while one was open for 2% of the time, Pallas kernels for 17%

profile of v6, /device:TPU:1, one launch (start us, length us, event | category | flops | bytes accessed | tf_op | source)
XLA Modules:
  0.0 61.3 jit_solution(4236364571649827690)
XLA Ops:
  0.0 1.0 %slice_select_fusion = (f32[5,64,128]{2,1,0:T(8,128)S(1)}, f32[5,64,128]{2,1,0:T(8,128)S(1)}) fusion(f32[240,64,128]{2,1,0:T(8,128)} %bitcast.13, pred[]{:T(512)S(6)} %eq.39), kind=kLoop, calls=%fused_computation.1 | loop fusion | flops 81920 | bytes 655361 | tf_op jit(solution)/shard_map/jit(_where)/select_n | solution.py:374
  1.0 0.7 %collective-permute-start.1 = (f32[5,64,128]{2,1,0:T(8,128)S(1)}, f32[5,64,128]{2,1,0:T(8,128)S(1)}, u32[]{:S(2)}, u32[]{:S(2)}) collective-permute-start(f32[5,64,128]{2,1,0:T(8,128)S(1)} %get-tuple-element.11), channel_id=1, source_target_pairs={{1,2},{2,1},{3,4},{4,3},{5,6},{6,5},{9,10},{10,9},{11,12},{12,11},... | collective-permute-start | bytes 491528 | tf_op jit(solution)/shard_map/ppermute | solution.py:374
  1.7 4.6 %collective-permute-start = (f32[5,64,128]{2,1,0:T(8,128)S(1)}, f32[5,64,128]{2,1,0:T(8,128)S(1)}, u32[]{:S(2)}, u32[]{:S(2)}) collective-permute-start(f32[5,64,128]{2,1,0:T(8,128)S(1)} %get-tuple-element.12), channel_id=1, source_target_pairs={{0,1},{1,0},{2,3},{3,2},{4,5},{5,4},{6,7},{7,6},{8,9},{9,8},{10,11... | collective-permute-start | bytes 491528 | tf_op jit(solution)/shard_map/ppermute | solution.py:373
  6.3 10.6 %residual_pool.1 = (f32[5,400,128]{2,1,0:T(8,128)S(1)}, s32[128]{0:T(128)S(1)}, f32[2,5,64,128]{3,2,1,0:T(8,128)S(1)}) custom-call(s32[1]{0:T(128)} %bitcast.2.myself, f32[5,5]{1,0:T(8,128)} %coupling.1, s32[128,128]{1,0:T(8,128)} %target.1, f32[5,48,64,128]{3,2,1,0:T(8,128)} %bitcast.14, f32[5,48,64,128]{3,2,1,0:T(8,128)} %bitcast.16, ...), custom_call_target="tpu_custom_call" | custom-call | flops 100000000 | bytes 27700000 | tf_op jit(solution)/shard_map/residual_pool/pallas_call | solution.py:223
  16.9 0.0 copy-start
  16.9 0.0 collective-permute-done.1.outer
  16.9 0.0 collective-permute-done.inner
  16.9 1.7 %edges_pack.1 = f32[4096,128]{1,0:T(8,128)} custom-call(s32[1]{0:T(128)} %bitcast.1.odd, s32[128]{0:T(128)S(1)} %get-tuple-element.8.slots, f32[5,400,128]{2,1,0:T(8,128)S(1)} %get-tuple-element.9.part, f32[2,5,64,128]{3,2,1,0:T(8,128)S(1)} %get-tuple-element.10.duals, f32[5,64,128]{2,1,0:T(8,128)S(1)} %collective-permute-done.inner, ...), custom_call_target="tpu_custom_call" | custom-call | flops 1000000 | bytes 3500000 | tf_op jit(solution)/shard_map/edges_pack/pallas_call | solution.py:294
  18.7 10.7 %all-to-all-start = ((f32[128,32,128]{2,1,0:T(8,128)}), f32[128,32,128]{2,1,0:T(8,128)S(1)}, u32[]{:S(2)}, u32[]{:S(2)}) async-start(f32[128,32,128]{2,1,0:T(8,128)} %bitcast.15), calls=%async_computation | async-start | bytes 4194304 | tf_op jit(solution)/shard_map/all_to_all | solution.py:381
  29.3 0.0 copy-done
  29.4 1.3 %select_reduce_fusion = s32[128]{0:T(128)S(1)} fusion(s32[16384]{0:T(1024)S(1)} %bitcast.20, s32[128]{0:T(128)S(1)} %iota_add_fusion), kind=kLoop, calls=%fused_computation | loop fusion | flops 6291328 | bytes 66560 | tf_op jit(solution)/shard_map/reduce_sum | solution.py:387
  30.7 0.2 convert_reduce_fusion
  30.9 28.8 %all-to-all-done = f32[128,32,128]{2,1,0:T(8,128)S(1)} async-done(((f32[128,32,128]{2,1,0:T(8,128)}), f32[128,32,128]{2,1,0:T(8,128)S(1)}, u32[]{:S(2)}, u32[]{:S(2)}) %all-to-all-start) | async-done | bytes 2097184 | tf_op jit(solution)/shard_map/all_to_all | solution.py:381
  59.7 1.6 %unpack.1 = f32[5,128,384]{2,1,0:T(8,128)} custom-call(s32[128]{0:T(128)S(1)} %multiply_add_fusion.lookup, f32[4096,128]{1,0:T(8,128)S(1)} %bitcast.12), custom_call_target="tpu_custom_call" | custom-call | bytes 3000000 | tf_op jit(solution)/shard_map/unpack/pallas_call | solution.py:339
  (3 shorter events, 0.0 us)
Async XLA Ops:
  1.0 15.9 %collective-permute-start.1 = (f32[5,64,128]{2,1,0:T(8,128)S(1)}, f32[5,64,128]{2,1,0:T(8,128)S(1)}, u32[]{:S(2)}, u32[]{:S(2)}) collective-permute-start(f32[5,64,128]{2,1,0:T(8,128)S(1)} %get-tuple-element.11), channel_id=1, source_target_pairs={{1,2},{2,1},{3,4},{4,3},{5,6},{6,5},{9,10},{10,9},{11,12},{12,11},... | collective-permute-start | bytes 491528 | tf_op jit(solution)/shard_map/ppermute | solution.py:374
  1.7 15.2 %collective-permute-start = (f32[5,64,128]{2,1,0:T(8,128)S(1)}, f32[5,64,128]{2,1,0:T(8,128)S(1)}, u32[]{:S(2)}, u32[]{:S(2)}) collective-permute-start(f32[5,64,128]{2,1,0:T(8,128)S(1)} %get-tuple-element.12), channel_id=1, source_target_pairs={{0,1},{1,0},{2,3},{3,2},{4,5},{5,4},{6,7},{7,6},{8,9},{9,8},{10,11... | collective-permute-start | bytes 491528 | tf_op jit(solution)/shard_map/ppermute | solution.py:373
  16.9 12.4 %copy-start = (s32[128,128]{1,0:T(8,128)S(1)}, s32[128,128]{1,0:T(8,128)}, u32[]{:S(2)}) copy-start(s32[128,128]{1,0:T(8,128)} %target.1) | copy-start | bytes 196612
  18.7 41.1 %all-to-all-start = ((f32[128,32,128]{2,1,0:T(8,128)}), f32[128,32,128]{2,1,0:T(8,128)S(1)}, u32[]{:S(2)}, u32[]{:S(2)}) async-start(f32[128,32,128]{2,1,0:T(8,128)} %bitcast.15), calls=%async_computation | async-start | bytes 4194304 | tf_op jit(solution)/shard_map/all_to_all | solution.py:381

commit v7 on v6

--- a/solution.py
+++ b/solution.py
@@ -256,6 +256,11 @@
     span = cells // per_dev
     kept = pe.shape[2] - 2 * PAD
     edge = edge_tiles(rows, span)
+    for t in range(edge, per_dev - edge):
+        values = tile_values(
+            lambda f, d: part[f, pl.ds(PAD + span * t + d, 8), :], fields, span, tile_rows, lanes
+        )
+        send_tile(slots[t], t, values, stage, out, tile_rows, sem.at[0])
     pv[...] = pool_matrix(lanes)
     swapped = odd[0] != 0
     for f in range(fields):
@@ -265,11 +270,6 @@
             wv[0, f, here, :] = duals[0, f, here, :] * jnp.where(swapped, near, far)
             wv[1, f, here, :] = duals[1, f, here, :] * jnp.where(swapped, far, near)
     pooled = [pooled_rows(wv.at[i], pv[...]) for i in range(2)]
-    for t in range(edge, per_dev - edge):
-        values = tile_values(
-            lambda f, d: part[f, pl.ds(PAD + span * t + d, 8), :], fields, span, tile_rows, lanes
-        )
-        send_tile(slots[t], t, values, stage, out, tile_rows, sem.at[0])
     for i, (at, start) in enumerate(((0, 0), (kept - rows, cells - kept))):
         for f in range(fields):
             pe[i, f, pl.ds(PAD, kept), :] = part[f, pl.ds(PAD + start, kept), :]

time: 61.6 us -> 61.6 us (level)
  no operation moved by 1% of the time
where the time goes in v7:
time: 61.6 us; the launch traced here: 61.3 us
  waiting for transfers between devices  28.8 us (47%)
  starting transfers between devices  15.9 us (26%)
  Pallas kernels  13.9 us (23%)
  other arithmetic  2.55 us (4%)
    all_to_all x1, waiting for transfers between devices, local(): incoming = lax.all_to_all(outgoing, ('grp', 'brk'), 0, 0, tiled=True)  28.8 us
    all_to_all x1, starting transfers between devices, local(): incoming = lax.all_to_all(outgoing, ('grp', 'brk'), 0, 0, tiled=True)  10.7 us
    pallas_call x1, Pallas kernels, main_part(): pl.pallas_call(functools.partial(main_kernel, capacity), out_shape=(jax.S...  10.6 us
    ppermute x1, starting transfers between devices, local(): inner = lax.ppermute(jnp.where(odd == 0, last, first), 'brk', one)  4.57 us
    pallas_call x1, Pallas kernels, pack_part(): pl.pallas_call(functools.partial(pack_kernel, tile_rows), out_shape=pltpu...  1.72 us
    pallas_call x1, Pallas kernels, unpack_part(): pl.pallas_call(functools.partial(unpack_kernel, tile_rows), out_shape=jax...  1.56 us
    reduce_sum x1, other arithmetic, local(): origin = jnp.sum(jnp.where(hit, codes[None, :], 0), axis=1)  1.32 us
  transfers between devices with their start and end apart: 3, of which 1 were waited for; matrix products, arithmetic and copies ran while one was open for 2% of the time, Pallas kernels for 17%

profile of v7, /device:TPU:1, one launch (start us, length us, event | category | flops | bytes accessed | tf_op | source)
XLA Modules:
  0.0 61.3 jit_solution(15526525735813313148)
XLA Ops:
  0.0 1.0 %slice_select_fusion = (f32[5,64,128]{2,1,0:T(8,128)S(1)}, f32[5,64,128]{2,1,0:T(8,128)S(1)}) fusion(f32[240,64,128]{2,1,0:T(8,128)} %bitcast.13, pred[]{:T(512)S(6)} %eq.39), kind=kLoop, calls=%fused_computation.1 | loop fusion | flops 81920 | bytes 655361 | tf_op jit(solution)/shard_map/jit(_where)/select_n | solution.py:374
  1.0 0.7 %collective-permute-start.1 = (f32[5,64,128]{2,1,0:T(8,128)S(1)}, f32[5,64,128]{2,1,0:T(8,128)S(1)}, u32[]{:S(2)}, u32[]{:S(2)}) collective-permute-start(f32[5,64,128]{2,1,0:T(8,128)S(1)} %get-tuple-element.11), channel_id=1, source_target_pairs={{1,2},{2,1},{3,4},{4,3},{5,6},{6,5},{9,10},{10,9},{11,12},{12,11},... | collective-permute-start | bytes 491528 | tf_op jit(solution)/shard_map/ppermute | solution.py:374
  1.7 4.6 %collective-permute-start = (f32[5,64,128]{2,1,0:T(8,128)S(1)}, f32[5,64,128]{2,1,0:T(8,128)S(1)}, u32[]{:S(2)}, u32[]{:S(2)}) collective-permute-start(f32[5,64,128]{2,1,0:T(8,128)S(1)} %get-tuple-element.12), channel_id=1, source_target_pairs={{0,1},{1,0},{2,3},{3,2},{4,5},{5,4},{6,7},{7,6},{8,9},{9,8},{10,11... | collective-permute-start | bytes 491528 | tf_op jit(solution)/shard_map/ppermute | solution.py:373
  6.3 10.6 %residual_pool.1 = (f32[5,400,128]{2,1,0:T(8,128)S(1)}, s32[128]{0:T(128)S(1)}, f32[2,5,64,128]{3,2,1,0:T(8,128)S(1)}) custom-call(s32[1]{0:T(128)} %bitcast.2.myself, f32[5,5]{1,0:T(8,128)} %coupling.1, s32[128,128]{1,0:T(8,128)} %target.1, f32[5,48,64,128]{3,2,1,0:T(8,128)} %bitcast.14, f32[5,48,64,128]{3,2,1,0:T(8,128)} %bitcast.16, ...), custom_call_target="tpu_custom_call" | custom-call | flops 100000000 | bytes 27700000 | tf_op jit(solution)/shard_map/residual_pool/pallas_call | solution.py:223
  16.9 0.0 copy-start
  16.9 0.0 collective-permute-done.1.outer
  16.9 0.0 collective-permute-done.inner
  16.9 1.7 %edges_pack.1 = f32[4096,128]{1,0:T(8,128)} custom-call(s32[1]{0:T(128)} %bitcast.1.odd, s32[128]{0:T(128)S(1)} %get-tuple-element.8.slots, f32[5,400,128]{2,1,0:T(8,128)S(1)} %get-tuple-element.9.part, f32[2,5,64,128]{3,2,1,0:T(8,128)S(1)} %get-tuple-element.10.duals, f32[5,64,128]{2,1,0:T(8,128)S(1)} %collective-permute-done.inner, ...), custom_call_target="tpu_custom_call" | custom-call | flops 1000000 | bytes 3500000 | tf_op jit(solution)/shard_map/edges_pack/pallas_call | solution.py:294
  18.7 10.7 %all-to-all-start = ((f32[128,32,128]{2,1,0:T(8,128)}), f32[128,32,128]{2,1,0:T(8,128)S(1)}, u32[]{:S(2)}, u32[]{:S(2)}) async-start(f32[128,32,128]{2,1,0:T(8,128)} %bitcast.15), calls=%async_computation | async-start | bytes 4194304 | tf_op jit(solution)/shard_map/all_to_all | solution.py:381
  29.4 0.0 copy-done
  29.4 1.3 %select_reduce_fusion = s32[128]{0:T(128)S(1)} fusion(s32[16384]{0:T(1024)S(1)} %bitcast.20, s32[128]{0:T(128)S(1)} %iota_add_fusion), kind=kLoop, calls=%fused_computation | loop fusion | flops 6291328 | bytes 66560 | tf_op jit(solution)/shard_map/reduce_sum | solution.py:387
  30.7 0.2 convert_reduce_fusion
  30.9 28.8 %all-to-all-done = f32[128,32,128]{2,1,0:T(8,128)S(1)} async-done(((f32[128,32,128]{2,1,0:T(8,128)}), f32[128,32,128]{2,1,0:T(8,128)S(1)}, u32[]{:S(2)}, u32[]{:S(2)}) %all-to-all-start) | async-done | bytes 2097184 | tf_op jit(solution)/shard_map/all_to_all | solution.py:381
  59.8 1.6 %unpack.1 = f32[5,128,384]{2,1,0:T(8,128)} custom-call(s32[128]{0:T(128)S(1)} %multiply_add_fusion.lookup, f32[4096,128]{1,0:T(8,128)S(1)} %bitcast.12), custom_call_target="tpu_custom_call" | custom-call | bytes 3000000 | tf_op jit(solution)/shard_map/unpack/pallas_call | solution.py:339
  (3 shorter events, 0.0 us)
Async XLA Ops:
  1.0 15.9 %collective-permute-start.1 = (f32[5,64,128]{2,1,0:T(8,128)S(1)}, f32[5,64,128]{2,1,0:T(8,128)S(1)}, u32[]{:S(2)}, u32[]{:S(2)}) collective-permute-start(f32[5,64,128]{2,1,0:T(8,128)S(1)} %get-tuple-element.11), channel_id=1, source_target_pairs={{1,2},{2,1},{3,4},{4,3},{5,6},{6,5},{9,10},{10,9},{11,12},{12,11},... | collective-permute-start | bytes 491528 | tf_op jit(solution)/shard_map/ppermute | solution.py:374
  1.7 15.2 %collective-permute-start = (f32[5,64,128]{2,1,0:T(8,128)S(1)}, f32[5,64,128]{2,1,0:T(8,128)S(1)}, u32[]{:S(2)}, u32[]{:S(2)}) collective-permute-start(f32[5,64,128]{2,1,0:T(8,128)S(1)} %get-tuple-element.12), channel_id=1, source_target_pairs={{0,1},{1,0},{2,3},{3,2},{4,5},{5,4},{6,7},{7,6},{8,9},{9,8},{10,11... | collective-permute-start | bytes 491528 | tf_op jit(solution)/shard_map/ppermute | solution.py:373
  16.9 12.5 %copy-start = (s32[128,128]{1,0:T(8,128)S(1)}, s32[128,128]{1,0:T(8,128)}, u32[]{:S(2)}) copy-start(s32[128,128]{1,0:T(8,128)} %target.1) | copy-start | bytes 196612
  18.7 41.1 %all-to-all-start = ((f32[128,32,128]{2,1,0:T(8,128)}), f32[128,32,128]{2,1,0:T(8,128)S(1)}, u32[]{:S(2)}, u32[]{:S(2)}) async-start(f32[128,32,128]{2,1,0:T(8,128)} %bitcast.15), calls=%async_computation | async-start | bytes 4194304 | tf_op jit(solution)/shard_map/all_to_all | solution.py:381

commit v8 on v7

--- a/solution.py
+++ b/solution.py
@@ -342,7 +342,7 @@
         in_specs=[pl.BlockSpec(memory_space=pltpu.SMEM), pl.BlockSpec(memory_space=pltpu.VMEM)],
         out_specs=pl.BlockSpec(memory_space=pltpu.HBM),
         scratch_shapes=[
-            pltpu.VMEM((4, 8 * (tile_rows + 1), lanes), jnp.float32),
+            pltpu.VMEM((per_dev // 8, 8 * (tile_rows + 1), lanes), jnp.float32),
             pltpu.VMEM((fields, per_dev, width), jnp.float32),
             pltpu.SemaphoreType.DMA((4,)),
         ],

time: 61.6 us -> 61.6 us (level)
  no operation moved by 1% of the time
where the time goes in v8:
time: 61.6 us; the launch traced here: 61.3 us
  waiting for transfers between devices  28.8 us (47%)
  starting transfers between devices  15.8 us (26%)
  Pallas kernels  13.9 us (23%)
  other arithmetic  2.55 us (4%)
    all_to_all x1, waiting for transfers between devices, local(): incoming = lax.all_to_all(outgoing, ('grp', 'brk'), 0, 0, tiled=True)  28.8 us
    pallas_call x1, Pallas kernels, main_part(): pl.pallas_call(functools.partial(main_kernel, capacity), out_shape=(jax.S...  10.6 us
    all_to_all x1, starting transfers between devices, local(): incoming = lax.all_to_all(outgoing, ('grp', 'brk'), 0, 0, tiled=True)  10.6 us
    ppermute x1, starting transfers between devices, local(): inner = lax.ppermute(jnp.where(odd == 0, last, first), 'brk', one)  4.57 us
    pallas_call x1, Pallas kernels, pack_part(): pl.pallas_call(functools.partial(pack_kernel, tile_rows), out_shape=pltpu...  1.73 us
    pallas_call x1, Pallas kernels, unpack_part(): pl.pallas_call(functools.partial(unpack_kernel, tile_rows), out_shape=jax...  1.56 us
    reduce_sum x1, other arithmetic, local(): origin = jnp.sum(jnp.where(hit, codes[None, :], 0), axis=1)  1.32 us
  transfers between devices with their start and end apart: 3, of which 1 were waited for; matrix products, arithmetic and copies ran while one was open for 2% of the time, Pallas kernels for 17%

profile of v8, /device:TPU:1, one launch (start us, length us, event | category | flops | bytes accessed | tf_op | source)
XLA Modules:
  0.0 61.3 jit_solution(4765248781760148598)
XLA Ops:
  0.0 1.0 %slice_select_fusion = (f32[5,64,128]{2,1,0:T(8,128)S(1)}, f32[5,64,128]{2,1,0:T(8,128)S(1)}) fusion(f32[240,64,128]{2,1,0:T(8,128)} %bitcast.13, pred[]{:T(512)S(6)} %eq.39), kind=kLoop, calls=%fused_computation.1 | loop fusion | flops 81920 | bytes 655361 | tf_op jit(solution)/shard_map/jit(_where)/select_n | solution.py:374
  1.0 0.7 %collective-permute-start.1 = (f32[5,64,128]{2,1,0:T(8,128)S(1)}, f32[5,64,128]{2,1,0:T(8,128)S(1)}, u32[]{:S(2)}, u32[]{:S(2)}) collective-permute-start(f32[5,64,128]{2,1,0:T(8,128)S(1)} %get-tuple-element.11), channel_id=1, source_target_pairs={{1,2},{2,1},{3,4},{4,3},{5,6},{6,5},{9,10},{10,9},{11,12},{12,11},... | collective-permute-start | bytes 491528 | tf_op jit(solution)/shard_map/ppermute | solution.py:374
  1.7 4.6 %collective-permute-start = (f32[5,64,128]{2,1,0:T(8,128)S(1)}, f32[5,64,128]{2,1,0:T(8,128)S(1)}, u32[]{:S(2)}, u32[]{:S(2)}) collective-permute-start(f32[5,64,128]{2,1,0:T(8,128)S(1)} %get-tuple-element.12), channel_id=1, source_target_pairs={{0,1},{1,0},{2,3},{3,2},{4,5},{5,4},{6,7},{7,6},{8,9},{9,8},{10,11... | collective-permute-start | bytes 491528 | tf_op jit(solution)/shard_map/ppermute | solution.py:373
  6.3 10.6 %residual_pool.1 = (f32[5,400,128]{2,1,0:T(8,128)S(1)}, s32[128]{0:T(128)S(1)}, f32[2,5,64,128]{3,2,1,0:T(8,128)S(1)}) custom-call(s32[1]{0:T(128)} %bitcast.2.myself, f32[5,5]{1,0:T(8,128)} %coupling.1, s32[128,128]{1,0:T(8,128)} %target.1, f32[5,48,64,128]{3,2,1,0:T(8,128)} %bitcast.14, f32[5,48,64,128]{3,2,1,0:T(8,128)} %bitcast.16, ...), custom_call_target="tpu_custom_call" | custom-call | flops 100000000 | bytes 27700000 | tf_op jit(solution)/shard_map/residual_pool/pallas_call | solution.py:223
  16.9 0.0 copy-start
  16.9 0.0 collective-permute-done.1.outer
  16.9 0.0 collective-permute-done.inner
  16.9 1.7 %edges_pack.1 = f32[4096,128]{1,0:T(8,128)} custom-call(s32[1]{0:T(128)} %bitcast.1.odd, s32[128]{0:T(128)S(1)} %get-tuple-element.8.slots, f32[5,400,128]{2,1,0:T(8,128)S(1)} %get-tuple-element.9.part, f32[2,5,64,128]{3,2,1,0:T(8,128)S(1)} %get-tuple-element.10.duals, f32[5,64,128]{2,1,0:T(8,128)S(1)} %collective-permute-done.inner, ...), custom_call_target="tpu_custom_call" | custom-call | flops 1000000 | bytes 3500000 | tf_op jit(solution)/shard_map/edges_pack/pallas_call | solution.py:294
  18.7 10.6 %all-to-all-start = ((f32[128,32,128]{2,1,0:T(8,128)}), f32[128,32,128]{2,1,0:T(8,128)S(1)}, u32[]{:S(2)}, u32[]{:S(2)}) async-start(f32[128,32,128]{2,1,0:T(8,128)} %bitcast.15), calls=%async_computation | async-start | bytes 4194304 | tf_op jit(solution)/shard_map/all_to_all | solution.py:381
  29.3 0.0 copy-done
  29.3 1.3 %select_reduce_fusion = s32[128]{0:T(128)S(1)} fusion(s32[16384]{0:T(1024)S(1)} %bitcast.20, s32[128]{0:T(128)S(1)} %iota_add_fusion), kind=kLoop, calls=%fused_computation | loop fusion | flops 6291328 | bytes 66560 | tf_op jit(solution)/shard_map/reduce_sum | solution.py:387
  30.6 0.2 convert_reduce_fusion
  30.9 28.8 %all-to-all-done = f32[128,32,128]{2,1,0:T(8,128)S(1)} async-done(((f32[128,32,128]{2,1,0:T(8,128)}), f32[128,32,128]{2,1,0:T(8,128)S(1)}, u32[]{:S(2)}, u32[]{:S(2)}) %all-to-all-start) | async-done | bytes 2097184 | tf_op jit(solution)/shard_map/all_to_all | solution.py:381
  59.7 1.6 %unpack.1 = f32[5,128,384]{2,1,0:T(8,128)} custom-call(s32[128]{0:T(128)S(1)} %multiply_add_fusion.lookup, f32[4096,128]{1,0:T(8,128)S(1)} %bitcast.12), custom_call_target="tpu_custom_call" | custom-call | bytes 3000000 | tf_op jit(solution)/shard_map/unpack/pallas_call | solution.py:339
  (3 shorter events, 0.0 us)
Async XLA Ops:
  1.0 15.9 %collective-permute-start.1 = (f32[5,64,128]{2,1,0:T(8,128)S(1)}, f32[5,64,128]{2,1,0:T(8,128)S(1)}, u32[]{:S(2)}, u32[]{:S(2)}) collective-permute-start(f32[5,64,128]{2,1,0:T(8,128)S(1)} %get-tuple-element.11), channel_id=1, source_target_pairs={{1,2},{2,1},{3,4},{4,3},{5,6},{6,5},{9,10},{10,9},{11,12},{12,11},... | collective-permute-start | bytes 491528 | tf_op jit(solution)/shard_map/ppermute | solution.py:374
  1.7 15.2 %collective-permute-start = (f32[5,64,128]{2,1,0:T(8,128)S(1)}, f32[5,64,128]{2,1,0:T(8,128)S(1)}, u32[]{:S(2)}, u32[]{:S(2)}) collective-permute-start(f32[5,64,128]{2,1,0:T(8,128)S(1)} %get-tuple-element.12), channel_id=1, source_target_pairs={{0,1},{1,0},{2,3},{3,2},{4,5},{5,4},{6,7},{7,6},{8,9},{9,8},{10,11... | collective-permute-start | bytes 491528 | tf_op jit(solution)/shard_map/ppermute | solution.py:373
  16.9 12.4 %copy-start = (s32[128,128]{1,0:T(8,128)S(1)}, s32[128,128]{1,0:T(8,128)}, u32[]{:S(2)}) copy-start(s32[128,128]{1,0:T(8,128)} %target.1) | copy-start | bytes 196612
  18.7 41.0 %all-to-all-start = ((f32[128,32,128]{2,1,0:T(8,128)}), f32[128,32,128]{2,1,0:T(8,128)S(1)}, u32[]{:S(2)}, u32[]{:S(2)}) async-start(f32[128,32,128]{2,1,0:T(8,128)} %bitcast.15), calls=%async_computation | async-start | bytes 4194304 | tf_op jit(solution)/shard_map/all_to_all | solution.py:381
